TPU v7x, 128 devices: a whole 4x4x4 slice. The times are simulated.
128 devices in a mesh: seq: 16 (over z_lo, x, core), db: 8 (over y, z_hi).
Axes of the slice: x: 4, y: 4, z: 4 (z_hi: 2, z_lo: 2; z = z_hi * 2 + z_lo), core: 2. Of those that a mesh axis runs over, the one named last changes fastest.
Arguments:
- hidden_in: bfloat16 [4096, 4096], P('seq'), may hold values from -4 to 4
- query_rows: bfloat16 [4096, 4096], P('seq', 'db'), may hold values from -32 to 32
- key_rows: bfloat16 [4096, 4096], P('seq', 'db'), may hold values from -32 to 32
- value_rows: bfloat16 [4096, 4096], P('seq', 'db'), may hold values from -6 to 6
- w_self_out: bfloat16 [4096, 4096], P('db'), may hold values from -0.1796875 to 0.1796875
- norm_gain: bfloat16 [4096], replicated, may hold values from 0.099609375 to 1.8984375
- w_cross_q: bfloat16 [4096, 4096], P(None, 'db'), may hold values from -2 to 2
- w_cross_k: bfloat16 [1024, 4096], P(None, 'db'), may hold values from -1 to 1
- w_cross_v: bfloat16 [1024, 4096], P(None, 'db'), may hold values from -0.1875 to 0.1875
- w_cross_out: bfloat16 [4096, 4096], P('db'), may hold values from -0.09375 to 0.09375
- enc_table: bfloat16 [64, 128, 1024], P('db'), may hold values from -6 to 6
- nb_shard: int32 [64, 2], P('seq'), may hold values from 0 to 7, all different within a row; in each aligned block of 4 rows (0 to 3, 4 to 7, ...) at most 2 rows name the same one
- nb_row: int32 [64, 2], P('seq'), may hold values from 0 to 7
Outputs:
- block_out: float32 [4096, 4096], P(('seq', 'db'))
Inputs may be any that keep to these rules, and one draw needn't show every extreme that they name: `nb_shard`: the spans held by one index of seq name each shard at most 2 times, and in the spans of some indices one shard exactly 2 times; the 2 neighbours of a span lie in different shards.
All inputs are finite; a program needn't handle non-finite values.
Results may differ from a plain program's by a relative error of at most 0.038.
Values may be sent and summed in bfloat16 or wider, within the bound.
A program may use at most 128 MiB of HBM per device.

v0:
```python
import math

import jax
import jax.numpy as jnp
from jax import lax
from jax.sharding import PartitionSpec as P

HD = 128
SPAN = 64
NEIGH = 2
NLEN = 128


NEG_BIG = -1e30


def from_behind(block, axis, distance):
    devices = range(lax.axis_size(axis))
    route = [(i - distance, i) for i in devices if i - distance in devices]
    return lax.ppermute(block, axis, route)


def attend_block(state, query_three, key_block, value_block, query_pos, key_pos, score_scale):
    run_max, run_sum, run_acc = state
    scores = (
        jnp.einsum("qhd,khd->hqk", query_three, key_block, preferred_element_type=jnp.float32)
        * score_scale
    )
    allowed = (key_pos[None, :] <= query_pos[:, None]) & (key_pos[None, :] >= 0)
    scores = jnp.where(allowed[None], scores, NEG_BIG)
    new_max = jnp.maximum(run_max, jnp.max(scores, axis=-1))
    rescale = jnp.exp(run_max - new_max)
    weights = jnp.exp(scores - new_max[..., None])
    new_sum = run_sum * rescale + jnp.sum(weights, axis=-1)
    added = jnp.einsum(
        "hqk,khd->hqd",
        weights.astype(jnp.bfloat16),
        value_block,
        preferred_element_type=jnp.float32,
    )
    return (new_max, new_sum, run_acc * rescale[..., None] + added)


def fold_piece(carried, query_three, pieces, query_pos, score_scale):
    key_piece, value_piece = pieces
    count_rows = key_piece.shape[0]
    heads_local = query_three.shape[1]
    block_rows = math.gcd(count_rows, 512)
    block_count = count_rows // block_rows
    last_query = query_pos[query_pos.shape[0] - 1]

    def one_block(block_index, state):
        key_first = block_index * block_rows

        def compute(inner):
            key_block = lax.dynamic_slice_in_dim(
                key_piece, block_index * block_rows, block_rows, 0
            ).reshape(block_rows, heads_local, HD)
            value_block = lax.dynamic_slice_in_dim(
                value_piece, block_index * block_rows, block_rows, 0
            ).reshape(block_rows, heads_local, HD)
            key_pos = key_first + jnp.arange(block_rows, dtype=jnp.int32)
            return attend_block(
                inner, query_three, key_block, value_block, query_pos, key_pos, score_scale
            )

        def unchanged(inner):
            return inner

        live = (key_first <= last_query) & (key_first + block_rows > 0)
        return lax.cond(live, compute, unchanged, state)

    return lax.fori_loop(0, block_count, one_block, carried)


def empty_state(heads_local, rows):
    return (
        jnp.full((heads_local, rows), NEG_BIG, jnp.float32),
        jnp.zeros((heads_local, rows), jnp.float32),
        jnp.zeros((heads_local, rows, HD), jnp.float32),
    )


def finish_state(state, rows, width_local):
    run_max, run_sum, run_acc = state
    return (
        (run_acc / run_sum[..., None])
        .transpose(1, 0, 2)
        .reshape(rows, width_local)
        .astype(jnp.bfloat16)
    )


def per_device(
    hidden_in,
    query_rows,
    key_rows,
    value_rows,
    w_self_out,
    norm_gain,
    w_cross_q,
    w_cross_k,
    w_cross_v,
    w_cross_out,
    enc_table,
    nb_shard,
    nb_row,
):
    tok_rows = hidden_in.shape[0]
    width_local = query_rows.shape[1]
    heads_local = width_local // HD
    db_count = lax.axis_size("db")
    seq_index = lax.axis_index("seq")
    db_index = lax.axis_index("db")
    score_scale = 1.0 / math.sqrt(HD)
    query_three = query_rows.reshape(tok_rows, heads_local, HD)
    query_pos = seq_index * tok_rows + jnp.arange(tok_rows, dtype=jnp.int32)
    initial = empty_state(heads_local, tok_rows)
    state = fold_piece(
        initial,
        query_three,
        (
            lax.all_gather(key_rows, "seq", axis=0, tiled=True),
            lax.all_gather(value_rows, "seq", axis=0, tiled=True),
        ),
        query_pos,
        score_scale,
    )
    attended = finish_state(state, tok_rows, width_local)
    share_rows = tok_rows // db_count
    attn_total = lax.psum(
        jnp.dot(attended, w_self_out, preferred_element_type=jnp.float32).astype(jnp.bfloat16), "db"
    ).astype(jnp.float32)
    residual = hidden_in.astype(jnp.float32) + attn_total
    mean_square = jnp.mean(residual * residual, axis=-1, keepdims=True)
    normed = (residual * lax.rsqrt(mean_square + 1e-05) * norm_gain.astype(jnp.float32)).astype(
        jnp.bfloat16
    )
    cross_query = jnp.dot(normed, w_cross_q, preferred_element_type=jnp.float32).astype(
        jnp.bfloat16
    )
    span_count = tok_rows // SPAN
    entry_count = span_count * NEIGH
    capacity = 2 * ((entry_count + db_count - 1) // db_count)
    shard_flat = nb_shard.reshape(entry_count)
    row_flat = nb_row.reshape(entry_count)
    entry_ids = jnp.arange(entry_count, dtype=jnp.int32)
    earlier = (shard_flat[:, None] == shard_flat[None, :]) & (
        entry_ids[None, :] < entry_ids[:, None]
    )
    rank_flat = jnp.sum(earlier.astype(jnp.int32), axis=1)
    slot_ids = jnp.arange(capacity, dtype=jnp.int32)
    chosen = ((shard_flat[None, :] == db_index) & (rank_flat[None, :] == slot_ids[:, None])).astype(
        jnp.int32
    )
    pick_rows = jnp.sum(chosen * row_flat[None, :], axis=1)
    live_slot = jnp.sum(chosen, axis=1) > 0
    picked = jnp.take(enc_table, pick_rows, axis=0)
    outgoing = jnp.where(live_slot[:, None, None], picked, jnp.zeros_like(picked))
    arrived = lax.all_gather(outgoing, "db", axis=0, tiled=True)
    wanted = jnp.take(arrived, shard_flat * capacity + rank_flat, axis=0).reshape(
        entry_count * NLEN, enc_table.shape[2]
    )
    cross_keys = jnp.dot(wanted, w_cross_k, preferred_element_type=jnp.float32).astype(jnp.bfloat16)
    cross_values = jnp.dot(wanted, w_cross_v, preferred_element_type=jnp.float32).astype(
        jnp.bfloat16
    )
    cross_pair = jnp.stack((cross_keys, cross_values)).reshape(
        2, span_count, NEIGH * NLEN, width_local
    )
    previous = from_behind(cross_pair[:, span_count - 1], "seq", 1)
    extended = jnp.concatenate((previous[:, None], cross_pair), axis=1).reshape(
        2, span_count + 1, NEIGH * NLEN, heads_local, HD
    )
    padded = jnp.pad(cross_query, ((1, SPAN - 1), (0, 0))).reshape(
        span_count + 1, SPAN, heads_local, HD
    )
    scores = (
        jnp.einsum("gqhd,gkhd->ghqk", padded, extended[0], preferred_element_type=jnp.float32)
        * score_scale
    )
    top_score = jnp.max(scores, axis=-1, keepdims=True)
    weights = jnp.exp(scores - top_score)
    totals = jnp.sum(weights, axis=-1, keepdims=True)
    mixed = (
        jnp.einsum(
            "ghqk,gkhd->ghqd",
            weights.astype(jnp.bfloat16),
            extended[1],
            preferred_element_type=jnp.float32,
        )
        / totals
    )
    cross_mixed = (
        mixed.transpose(0, 2, 1, 3)
        .reshape((span_count + 1) * SPAN, width_local)[1 : tok_rows + 1]
        .astype(jnp.bfloat16)
    )
    cross_share = lax.psum_scatter(
        jnp.dot(cross_mixed, w_cross_out, preferred_element_type=jnp.float32).astype(jnp.bfloat16),
        "db",
        scatter_dimension=0,
        tiled=True,
    ).astype(jnp.float32)
    own_residual = lax.dynamic_slice_in_dim(residual, db_index * share_rows, share_rows, 0)
    return own_residual + cross_share


def solution(mesh):
    placed = (
        P("seq", None),
        P("seq", "db"),
        P("seq", "db"),
        P("seq", "db"),
        P("db", None),
        P(),
        P(None, "db"),
        P(None, "db"),
        P(None, "db"),
        P("db", None),
        P("db", None, None),
        P("seq", None),
        P("seq", None),
    )
    return jax.shard_map(
        per_device, mesh=mesh, in_specs=placed, out_specs=P(("seq", "db"), None), check_vma=False
    )
```

profile of v0, /device:TPU:0, one launch (start us, length us, event | category | flops | bytes accessed | tf_op | source)
XLA Modules:
  0.0 419.2 jit_solution(12266112979966981673)
XLA Ops:
  6.6 0.9 copy.65
  7.5 0.1 mul.94
  7.6 0.8 copy.64
  8.3 0.1 reshape.166
  8.4 0.2 convert_reduce_fusion
  8.6 0.1 convert_reduce_fusion.1
  8.8 0.6 gather_fusion
  9.4 0.9 select_select_fusion
  10.3 0.0 all-gather.8.cloned.1.call-update
  10.4 0.0 all-gather.4.cloned.1.call-start
  10.4 0.8 copy.59
  11.3 0.0 all-gather.4.cloned.1.call-update
  11.3 0.0 all-gather.6.cloned.1.call-start
  11.3 0.8 copy.61
  12.2 0.0 all-gather.6.cloned.1.call-update
  12.2 0.0 all-reduce.3.cloned.1.call-start
  12.3 0.1 copy.66
  12.4 0.1 mul.98
  12.5 0.7 slice.18
  13.1 0.1 copy.60
  13.3 0.2 copy.62
  13.5 0.1 broadcast_bitcast_fusion
  13.5 71.1 %all-gather.8.cloned.1.call-done = bf16[16,128,1024]{2,1,0:T(8,128)(2,1)} async-done(((bf16[2,128,1024]{2,1,0:T(8,128)(2,1)}), bf16[16,128,1024]{2,1,0:T(8,128)(2,1)}) %all-gather.8.cloned.1.call-update) | async-done | bytes 4194320 | tf_op jit(solution)/shard_map/all_gather | solution.py:160
  84.6 2.9 gather_fusion.1
  87.5 41.5 %all-gather.4.cloned.1.call-done = bf16[4096,512]{0,1:T(8,128)(2,1)} async-done(((bf16[256,512]{0,1:T(8,128)(2,1)}), bf16[4096,512]{0,1:T(8,128)(2,1)}) %all-gather.4.cloned.1.call-update) | async-done | bytes 4194320 | tf_op jit(solution)/shard_map/all_gather | solution.py:123
  129.0 46.8 %all-gather.6.cloned.1.call-done = bf16[4096,512]{0,1:T(8,128)(2,1)} async-done(((bf16[256,512]{0,1:T(8,128)(2,1)}), bf16[4096,512]{0,1:T(8,128)(2,1)}) %all-gather.6.cloned.1.call-update) | async-done | bytes 4194320 | tf_op jit(solution)/shard_map/all_gather | solution.py:124
  175.8 8.5 %while.18 = (s32[]{:T(128)}, f32[4,256]{1,0:T(4,128)S(1)}, f32[4,256]{1,0:T(4,128)S(1)}, f32[4,256,128]{2,1,0:T(8,128)S(1)}, s32[]{:T(128)}, /*index=5*/bf16[409...) while((s32[]{:T(128)}, f32[4,256]{1,0:T(4,128)S(1)}, ...), condition=%wide.region_5.6_spmd.clone, body=%wide.region_0.5_spmd.clone.sunk | while | flops 272633600 | bytes 11085173 | solution.py:73
  176.4 3.1 conditional.3
  176.5 0.2 compare_and_fusion
  176.7 1.3 constant_dynamic-slice_fusion
  178.0 0.6 fusion.22
  178.6 0.3 fusion.3
  178.9 0.6 convolution_add_fusion
  184.3 0.2 copy.63
  184.6 4.8 %convolution_convert_fusion.1 = bf16[256,4096]{1,0:T(8,128)(2,1)} fusion(bf16[256,512]{0,1:T(8,128)(2,1)S(1)} %bitcast.62, bf16[512,4096]{1,0:T(8,128)(2,1)} %param.21), kind=kOutput, calls=%fused_computation.18 | convolution fusion | flops 1074790400 | bytes 6553600 | tf_op jit(solution)/shard_map/dot_general | solution.py:132
  189.4 0.0 all-reduce.3.cloned.1.call-update
  189.4 0.0 reduce-scatter.2.cloned.1.call-start
  189.5 0.4 bitcast_select_fusion.1
  189.9 0.8 copy-done.12
  190.7 1.2 convolution_convert_fusion.3
  191.9 0.1 copy-done.4
  192.0 0.5 copy.67
  192.5 3.1 convolution_convert_fusion.2
  195.6 0.5 copy.68
  196.1 0.1 fusion.16
  196.2 2.4 collective-permute-start
  198.6 1.3 collective-permute-done
  199.9 0.3 maximum_maximum_fusion
  200.2 0.2 fusion.23
  200.4 121.6 %all-reduce.3.cloned.1.call-done = bf16[256,4096]{1,0:T(8,128)(2,1)} async-done(((bf16[256,4096]{1,0:T(8,128)(2,1)}), bf16[256,4096]{1,0:T(8,128)(2,1)}) %all-reduce.3.cloned.1.call-update) | async-done | bytes 2097168 | tf_op jit(solution)/shard_map/psum | solution.py:131
  322.0 5.2 %convert_add_fusion = (f32[256,4096]{1,0:T(8,128)}, f32[256]{0:T(256)S(1)}) fusion(bf16[256,4096]{1,0:T(8,128)(2,1)} %all-reduce.3.cloned.1.call-done, bf16[256,4096]{1,0:T(8,128)(2,1)} %param.17), kind=kLoop, calls=%fused_computation.21 | loop fusion | flops 5242624 | bytes 8389632 | tf_op jit(solution)/shard_map/add | solution.py:134
  327.2 1.0 copy-done.10
  328.2 1.3 fusion.11
  329.5 0.1 pad.4
  329.6 0.1 reshape.165
  329.7 0.4 fusion.24
  330.1 0.5 fusion.12
  330.6 0.7 fusion.10
  331.2 0.3 copy.73
  331.6 1.2 copy-done.11
  332.8 2.6 convolution_convert_fusion
  335.4 0.0 reduce-scatter.2.cloned.1.call-update
  335.4 75.3 %reduce-scatter.2.cloned.1.call-done = bf16[32,4096]{1,0:T(8,128)(2,1)} async-done(((bf16[256,4096]{1,0:T(8,128)(2,1)}), bf16[32,4096]{1,0:T(8,128)(2,1)}) %reduce-scatter.2.cloned.1.call-update) | async-done | bytes 262160 | tf_op jit(solution)/shard_map/reduce_scatter | solution.py:199
  410.7 2.0 convert_add_fusion.1
  (59 shorter events, 0.4 us)
Async XLA Ops:
  6.5 2.3 copy-start
  6.5 3.9 copy-start.5
  6.5 4.8 %copy-start.6 = (bf16[256,512]{1,0:T(8,128)(2,1)S(1)}, bf16[256,512]{1,0:T(8,128)(2,1)}, u32[]{:S(2)}) copy-start(bf16[256,512]{1,0:T(8,128)(2,1)} %param.20) | copy-start | bytes 786436
  6.5 78.1 %all-gather.8.cloned.1.call-start = ((), (), s32[]{:S(2)}) async-start(), calls=%async_computation.4 | async-start | bytes 4718592 | tf_op jit(solution)/shard_map/all_gather | solution.py:160
  8.8 3.5 copy-start.9
  8.8 4.3 %copy-start.7 = (bf16[256,512]{1,0:T(8,128)(2,1)S(1)}, bf16[256,512]{1,0:T(8,128)(2,1)}, u32[]{:S(2)}) copy-start(bf16[256,512]{1,0:T(8,128)(2,1)} %param.18) | copy-start | bytes 786436
  10.4 118.6 %all-gather.4.cloned.1.call-start = ((), (), s32[]{:S(2)}) async-start(), calls=%async_computation.1 | async-start | bytes 4456448 | tf_op jit(solution)/shard_map/all_gather | solution.py:123
  11.3 164.5 %all-gather.6.cloned.1.call-start = ((), (), s32[]{:S(2)}) async-start(), calls=%async_computation.2 | async-start | bytes 4456448 | tf_op jit(solution)/shard_map/all_gather | solution.py:124
  12.2 309.8 %all-reduce.3.cloned.1.call-start = ((), (), s32[]{:S(2)}) async-start(), calls=%async_computation.3 | async-start | bytes 4194304 | tf_op jit(solution)/shard_map/psum | solution.py:131
  189.4 1.2 copy-start.12
  189.4 221.3 %reduce-scatter.2.cloned.1.call-start = ((), (), s32[]{:S(2)}) async-start(), calls=%async_computation.5 | async-start | bytes 2359296 | tf_op jit(solution)/shard_map/reduce_scatter | solution.py:199
  190.7 1.3 copy-start.4
  195.6 3.0 copy-start.8
  196.2 3.7 collective-permute-start
  322.0 5.2 %copy-start.2 = (bf16[256,4096]{1,0:T(8,128)(2,1)S(1)}, bf16[256,4096]{1,0:T(8,128)(2,1)}, u32[]{:S(2)}) copy-start(bf16[256,4096]{1,0:T(8,128)(2,1)} %param.17) | copy-start | bytes 6291460
  322.0 5.2 %copy-start.3 = (bf16[256,4096]{1,0:T(8,128)(2,1)S(1)}, bf16[256,4096]{1,0:T(8,128)(2,1)}, u32[]{:S(2)}) copy-start(bf16[256,4096]{1,0:T(8,128)(2,1)} %all-reduce.3.cloned.1.call-done) | copy-start | bytes 6291460
  322.0 6.2 %copy-start.10 = (bf16[4096,512]{1,0:T(8,128)(2,1)S(1)}, bf16[4096,512]{1,0:T(8,128)(2,1)}, u32[]{:S(2)}) copy-start(bf16[4096,512]{1,0:T(8,128)(2,1)} %param.23) | copy-start | bytes 12582916
  330.6 2.2 copy-start.11
  332.8 79.9 %copy-start.1 = (bf16[8,128,1024]{2,1,0:T(8,128)(2,1)S(1)}, bf16[8,128,1024]{2,1,0:T(8,128)(2,1)}, u32[]{:S(2)}) copy-start(bf16[8,128,1024]{2,1,0:T(8,128)(2,1)} %param.27) | copy-start | bytes 6291460
Sparse Core Ops, SparseCore 0:
  10.5 74.0 all-gather.7
  86.2 42.6 all-gather.3
  130.6 45.1 all-gather.5
  189.5 132.3 all-reduce.2
  335.5 75.1 reduce-scatter.1
where the time goes:
time: 420 us; the launch traced here: 419 us
  waiting for transfers between devices  358 us (85%)
  matrix products  15.3 us (4%)
  local copies, waits for them, and re-layouts  14.5 us (3%)
  between operations  13.5 us (3%)
  other arithmetic  10.3 us (2%)
  loops' own time  5.49 us (1%)
    psum x1, waiting for transfers between devices, per_device(): lax.psum(jnp.dot(attended, w_self_out, preferred_element_type=jnp.float32...  122 us
    reduce_scatter x1, waiting for transfers between devices, per_device(): lax.psum_scatter(jnp.dot(cross_mixed, w_cross_out, preferred_element_type...  75.3 us
    all_gather x1, waiting for transfers between devices, per_device(): arrived = lax.all_gather(outgoing, 'db', axis=0, tiled=True)  71.1 us
    all_gather x1, waiting for transfers between devices, per_device(): lax.all_gather(value_rows, 'seq', axis=0, tiled=True)  46.8 us
    all_gather x1, waiting for transfers between devices, per_device(): lax.all_gather(key_rows, 'seq', axis=0, tiled=True)  41.5 us
  transfers between devices with their start and end apart: 6, of which 6 were waited for; matrix products, arithmetic and copies ran while one was open for 3% of the time, Pallas kernels for 0%

commit v1 on v0

v1 whole, which is shorter than its diff:
```python
import functools
import math

import jax
import jax.numpy as jnp
from jax import lax
from jax.experimental import pallas as pl
from jax.experimental.pallas import tpu as pltpu
from jax.sharding import PartitionSpec as P

HD = 128
SPAN = 64
NLEN = 128
TOK = 256
WIDTH = 512
D = 4096
SHARE = 32
NEG_BIG = -1e30
MESH = pl.DeviceIdType.MESH
EXP2_SCALE = math.log2(math.e) / math.sqrt(HD)
BF16 = jnp.bfloat16
F32 = jnp.float32


def remote(src, dst, send, recv, seq, db):
    return pltpu.make_async_remote_copy(
        src_ref=src, dst_ref=dst, send_sem=send, recv_sem=recv, device_id=(seq, db), device_id_type=MESH
    )


def dot_f32(a, b):
    return jnp.dot(a, b, preferred_element_type=F32)


def dot_nt(a, b):
    return lax.dot_general(a, b, (((1,), (1,)), ((), ())), preferred_element_type=F32)


def block_kernel(
    q_ref,
    k_ref,
    v_ref,
    gain_ref,
    shard_ref,
    row_ref,
    hidden_hbm,
    wso_hbm,
    wcq_hbm,
    wck_hbm,
    wcv_hbm,
    wco_hbm,
    enc_hbm,
    out_ref,
    wso,
    wcq,
    wck,
    wcv,
    wco,
    enc,
    hid,
    kvs,
    qst,
    kv,
    qb,
    ob,
    ret,
    sc_buf,
    lsum,
    acc,
    att,
    enc_out,
    arr,
    part,
    rs1,
    rs2,
    res,
    nf,
    cqa,
    qx,
    kx,
    vx,
    wsem,
    xs,
    xr,
    zs,
    zr,
    cs,
    cr,
    qs,
    qr,
    os_,
    or_,
    es,
    er,
    r1s,
    r1r,
    ags,
    agr,
    r2s,
    r2r,
    ps,
    pr,
):
    s = lax.axis_index("seq")
    d = lax.axis_index("db")
    c = s % 2
    x = (s // 2) % 4
    zl = s // 8

    def at(zz, xx, cc):
        return (zz * 4 + xx) * 2 + cc

    own_rows = pl.ds(pl.multiple_of(d * SHARE, SHARE), SHARE)

    bar = pltpu.get_barrier_semaphore()
    for step in range(1, 16):
        pl.semaphore_signal(bar, inc=1, device_id=((s + step) % 16, d), device_id_type=MESH)
    for step in range(1, 8):
        pl.semaphore_signal(bar, inc=1, device_id=(s, (d + step) % 8), device_id_type=MESH)

    loads = [
        pltpu.make_async_copy(enc_hbm, enc, wsem.at[0]),
        pltpu.make_async_copy(wso_hbm, wso, wsem.at[1]),
        pltpu.make_async_copy(hidden_hbm.at[own_rows], hid, wsem.at[2]),
        pltpu.make_async_copy(wck_hbm, wck, wsem.at[3]),
        pltpu.make_async_copy(wcv_hbm, wcv, wsem.at[4]),
        pltpu.make_async_copy(wcq_hbm, wcq, wsem.at[5]),
        pltpu.make_async_copy(wco_hbm, wco, wsem.at[6]),
    ]
    for load in loads:
        load.start()
    for h in range(4):
        cols = slice(h * HD, (h + 1) * HD)
        kvs[h, 0] = k_ref[:, cols]
        kvs[h, 1] = v_ref[:, cols]
        qst[h] = q_ref[:, cols]
    pl.semaphore_wait(bar, 22)

    sends = []

    def start(copy):
        copy.start()
        sends.append(copy)

    for dx in (1, 3, 2):
        other = (x + dx) % 4
        start(remote(kvs.at[other], kv.at[s], xs.at[dx], xr.at[dx], at(zl, other, c), d))
    kv[s] = kvs[x]
    low = s % 8
    high = low // 4
    j_to = (1 - high) * low + high * (7 - low)
    slot_to = (s // 8) * 2 + high
    for h in range(4):
        goal = at(j_to // 2, h, j_to % 2)

        @pl.when(goal != s)
        def _():
            remote(qst.at[h], qb.at[slot_to], qs.at[h], qr.at[slot_to], goal, d).start()

        @pl.when(goal == s)
        def _():
            pltpu.make_async_copy(qst.at[h], qb.at[slot_to], qr.at[slot_to]).start()

    loads[0].wait()
    first = jnp.int32(0)
    second = jnp.int32(0)
    found = jnp.int32(0)
    for e in range(8):
        match = shard_ref[e // 2, e % 2] == d
        row = row_ref[e // 2, e % 2]
        first = jnp.where(match & (found == 0), row, first)
        second = jnp.where(match & (found == 1), row, second)
        found = found + match.astype(jnp.int32)
    enc_out[0] = enc[first]
    enc_out[1] = enc[second]

    def forward(src, k):
        start(remote(kv.at[src], kv.at[src], zs.at[k], zr.at[k], at(1 - zl, x, c), d))
        start(remote(kv.at[src], kv.at[src], cs.at[k], cr.at[k], at(zl, x, 1 - c), d))

    forward(s, 0)
    for dx in (1, 3, 2):
        src = at(zl, (x - dx + 4) % 4, c)
        remote(kv.at[src], kv.at[src], xs.at[dx], xr.at[dx], src, d).wait_recv()
        forward(src, dx)
    for dd in (1, 7, 2, 6, 3, 5, 4):
        start(
            remote(enc_out, arr.at[pl.ds(2 * d, 2)], es.at[dd], er.at[dd], s, (d + dd) % 8)
        )
    arr[2 * d] = enc_out[0]
    arr[2 * d + 1] = enc_out[1]
    for dx in (0, 1, 3, 2):
        src = at(1 - zl, (x - dx + 4) % 4, c)
        remote(kv.at[src], kv.at[src], zs.at[dx], zr.at[dx], src, d).wait_recv()
        start(remote(kv.at[src], kv.at[src], cs.at[4 + dx], cr.at[4 + dx], at(zl, x, 1 - c), d))
    for zz in range(2):
        for dx in range(4):
            src = at((zl + zz) % 2, (x - dx + 4) % 4, 1 - c)
            k = 4 * zz + dx
            remote(kv.at[src], kv.at[src], cs.at[k], cr.at[k], src, d).wait_recv()

    j = zl * 2 + c

    def block_of(i):
        return (i // 2) * 8 + (i % 2) * (7 - j) + (1 - i % 2) * j

    def slot(i, carry):
        b = block_of(i)
        remote(qst.at[0], qb.at[i], qs.at[0], qr.at[i], s, d).wait_recv()
        query = qb[i]
        last = (b + 2) // 2 - 1

        def lanes_max(scores):
            return jnp.maximum(
                jnp.maximum(scores[:, 0:128], scores[:, 128:256]),
                jnp.maximum(scores[:, 256:384], scores[:, 384:512]),
            )

        def first_pass(kb, top):
            keys = kv[pl.ds(2 * kb, 2), 0].reshape(512, HD)
            scores = dot_nt(query, keys)
            sc_buf[kb] = scores
            return jnp.maximum(top, lanes_max(scores))

        top = lax.fori_loop(0, last, first_pass, jnp.full((TOK, 128), NEG_BIG, F32))
        keys = kv[pl.ds(2 * last, 2), 0].reshape(512, HD)
        scores = dot_nt(query, keys)
        key_pos = last * 512 + lax.broadcasted_iota(jnp.int32, (TOK, 512), 1)
        query_pos = b * TOK + lax.broadcasted_iota(jnp.int32, (TOK, 512), 0)
        scores = jnp.where(key_pos <= query_pos, scores, NEG_BIG)
        sc_buf[last] = scores
        top = jnp.max(jnp.maximum(top, lanes_max(scores)), axis=-1, keepdims=True)
        lsum[...] = jnp.zeros_like(lsum)
        acc[...] = jnp.zeros_like(acc)

        def second_pass(kb, carry):
            weights = jnp.exp2((sc_buf[kb] - top) * EXP2_SCALE)
            values = kv[pl.ds(2 * kb, 2), 1].reshape(512, HD)
            lsum[...] += (weights[:, 0:128] + weights[:, 128:256]) + (
                weights[:, 256:384] + weights[:, 384:512]
            )
            acc[...] += dot_f32(weights.astype(BF16), values)
            return carry

        lax.fori_loop(0, last + 1, second_pass, 0)
        total = jnp.sum(lsum[...], axis=-1, keepdims=True)
        ob[i] = (acc[...] / total).astype(BF16)

        @pl.when(b != s)
        def _():
            remote(ob.at[i], ret.at[x], os_.at[i], or_.at[x], b, d).start()

        @pl.when(b == s)
        def _():
            pltpu.make_async_copy(ob.at[i], ret.at[x], or_.at[x]).start()

        return carry

    lax.fori_loop(0, 4, slot, 0)
    for h in range(4):
        remote(ob.at[0], ret.at[h], os_.at[0], or_.at[h], s, d).wait_recv()
        att[:, h * HD : (h + 1) * HD] = ret[h]

    def project(lhs, weight):
        def tile(n, carry):
            cols = pl.ds(pl.multiple_of(n * 512, 512), 512)
            part[:, cols] = dot_f32(lhs, weight[:, cols]).astype(BF16)
            return carry

        lax.fori_loop(0, 8, tile, 0)

    loads[1].wait()
    project(att[...], wso)
    spread = []
    for dd in (4, 3, 5, 2, 6, 1, 7):
        other = (d + dd) % 8
        rows = pl.ds(pl.multiple_of(other * SHARE, SHARE), SHARE)
        copy = remote(part.at[rows], rs1.at[dd], r1s.at[dd], r1r.at[dd], s, other)
        copy.start()
        spread.append(copy)

    for dd in range(1, 8):
        src = (d - dd + 8) % 8
        remote(enc_out, arr.at[pl.ds(2 * src, 2)], es.at[dd], er.at[dd], s, src).wait_recv()
    loads[3].wait()
    loads[4].wait()
    for e in range(8):
        shard = shard_ref[e // 2, e % 2]
        rank = jnp.int32(0)
        for earlier in range(e):
            rank = rank + (shard_ref[earlier // 2, earlier % 2] == shard).astype(jnp.int32)
        entry = arr[shard * 2 + rank]
        rows = slice((e % 2) * NLEN, (e % 2 + 1) * NLEN)
        kx[e // 2 + 1, rows, :] = dot_f32(entry, wck[...]).astype(BF16)
        vx[e // 2 + 1, rows, :] = dot_f32(entry, wcv[...]).astype(BF16)

    @pl.when(s < 15)
    def _():
        remote(kx.at[4], kx.at[0], ps.at[0], pr.at[0], s + 1, d).start()
        remote(vx.at[4], vx.at[0], ps.at[1], pr.at[1], s + 1, d).start()

    @pl.when(s == 0)
    def _():
        kx[0] = jnp.zeros((2 * NLEN, WIDTH), BF16)
        vx[0] = jnp.zeros((2 * NLEN, WIDTH), BF16)

    loads[2].wait()
    for dd in range(1, 8):
        remote(part.at[own_rows], rs1.at[dd], r1s.at[dd], r1r.at[dd], s, d).wait_recv()

    def add_up(n, square):
        cols = pl.ds(pl.multiple_of(n * 512, 512), 512)
        total = part[own_rows, cols].astype(F32)
        for dd in range(1, 8):
            total = total + rs1[dd, :, cols].astype(F32)
        total = total + hid[:, cols].astype(F32)
        res[:, cols] = total
        return square + total * total

    square = lax.fori_loop(0, 8, add_up, jnp.zeros((SHARE, 512), F32))
    scale = lax.rsqrt(jnp.sum(square, axis=-1, keepdims=True) / D + 1e-05)

    def normalise(n, carry):
        cols = pl.ds(pl.multiple_of(n * 512, 512), 512)
        nf[own_rows, cols] = (res[:, cols] * scale * gain_ref[:, cols].astype(F32)).astype(BF16)
        return carry

    lax.fori_loop(0, 8, normalise, 0)
    for dd in (4, 3, 5, 2, 6, 1, 7):
        start(
            remote(nf.at[own_rows], nf.at[own_rows], ags.at[dd], agr.at[dd], s, (d + dd) % 8)
        )
    for copy in spread:
        copy.wait_send()
    loads[5].wait()
    for dd in range(1, 8):
        src = (d - dd + 8) % 8
        rows = pl.ds(pl.multiple_of(src * SHARE, SHARE), SHARE)
        remote(nf.at[rows], nf.at[rows], ags.at[dd], agr.at[dd], s, src).wait_recv()

    cqa[...] = jnp.zeros_like(cqa)

    def contract(n, carry):
        cols = pl.ds(pl.multiple_of(n * 512, 512), 512)
        cqa[...] += dot_f32(nf[:, cols], wcq[cols, :])
        return carry

    lax.fori_loop(0, 8, contract, 0)
    qx[...] = pltpu.roll(cqa[...].astype(BF16).astype(F32), 1, 0).astype(BF16)

    @pl.when(s > 0)
    def _():
        remote(kx.at[4], kx.at[0], ps.at[0], pr.at[0], s, d).wait_recv()
        remote(vx.at[4], vx.at[0], ps.at[1], pr.at[1], s, d).wait_recv()

    def attend(query, keys, values):
        scores = dot_nt(query, keys)
        top = jnp.max(scores, axis=-1, keepdims=True)
        weights = jnp.exp2((scores - top) * EXP2_SCALE)
        total = jnp.sum(weights, axis=-1, keepdims=True)
        return dot_f32(weights.astype(BF16), values) / total

    def group(g, carry):
        rows = pl.ds(pl.multiple_of(g * SPAN, SPAN), SPAN)
        for h in range(4):
            cols = slice(h * HD, (h + 1) * HD)
            cqa[rows, cols] = attend(qx[rows, cols], kx[g, :, cols], vx[g, :, cols])
        return carry

    lax.fori_loop(0, 4, group, 0)
    for h in range(4):
        cols = slice(h * HD, (h + 1) * HD)
        tail = attend(qx[0:16, cols], kx[4, :, cols], vx[4, :, cols])
        first_row = lax.broadcasted_iota(jnp.int32, (16, HD), 0) == 0
        cqa[0:16, cols] = jnp.where(first_row, tail, cqa[0:16, cols])
    att[...] = pltpu.roll(cqa[...], TOK - 1, 0).astype(BF16)

    loads[6].wait()
    project(att[...], wco)
    for dd in (4, 3, 5, 2, 6, 1, 7):
        other = (d + dd) % 8
        rows = pl.ds(pl.multiple_of(other * SHARE, SHARE), SHARE)
        start(remote(part.at[rows], rs2.at[dd], r2s.at[dd], r2r.at[dd], s, other))
    for dd in range(1, 8):
        remote(part.at[own_rows], rs2.at[dd], r2s.at[dd], r2r.at[dd], s, d).wait_recv()

    def finish(n, carry):
        cols = pl.ds(pl.multiple_of(n * 512, 512), 512)
        total = part[own_rows, cols].astype(F32)
        for dd in range(1, 8):
            total = total + rs2[dd, :, cols].astype(F32)
        out_ref[:, cols] = res[:, cols] + total
        return carry

    lax.fori_loop(0, 8, finish, 0)

    for copy in sends:
        copy.wait_send()
    for h in range(4):
        goal = at(j_to // 2, h, j_to % 2)

        @pl.when(goal != s)
        def _():
            remote(qst.at[h], qb.at[0], qs.at[h], qr.at[0], goal, d).wait_send()

    for i in range(4):

        @pl.when(block_of(i) != s)
        def _():
            remote(ob.at[i], ret.at[0], os_.at[i], or_.at[0], s, d).wait_send()

    @pl.when(s < 15)
    def _():
        remote(kx.at[4], kx.at[0], ps.at[0], pr.at[0], s, d).wait_send()
        remote(vx.at[4], vx.at[0], ps.at[1], pr.at[1], s, d).wait_send()


def per_device(
    hidden_in,
    query_rows,
    key_rows,
    value_rows,
    w_self_out,
    norm_gain,
    w_cross_q,
    w_cross_k,
    w_cross_v,
    w_cross_out,
    enc_table,
    nb_shard,
    nb_row,
):
    vmem = pl.BlockSpec(memory_space=pltpu.VMEM)
    smem = pl.BlockSpec(memory_space=pltpu.SMEM)
    hbm = pl.BlockSpec(memory_space=pl.ANY)
    scratch = [
        pltpu.VMEM((WIDTH, D), BF16),
        pltpu.VMEM((D, WIDTH), BF16),
        pltpu.VMEM((1024, WIDTH), BF16),
        pltpu.VMEM((1024, WIDTH), BF16),
        pltpu.VMEM((WIDTH, D), BF16),
        pltpu.VMEM((8, NLEN, 1024), BF16),
        pltpu.VMEM((SHARE, D), BF16),
        pltpu.VMEM((4, 2, TOK, HD), BF16),
        pltpu.VMEM((4, TOK, HD), BF16),
        pltpu.VMEM((16, 2, TOK, HD), BF16),
        pltpu.VMEM((4, TOK, HD), BF16),
        pltpu.VMEM((4, TOK, HD), BF16),
        pltpu.VMEM((4, TOK, HD), BF16),
        pltpu.VMEM((8, TOK, 512), F32),
        pltpu.VMEM((TOK, HD), F32),
        pltpu.VMEM((TOK, HD), F32),
        pltpu.VMEM((TOK, WIDTH), BF16),
        pltpu.VMEM((2, NLEN, 1024), BF16),
        pltpu.VMEM((16, NLEN, 1024), BF16),
        pltpu.VMEM((TOK, D), BF16),
        pltpu.VMEM((8, SHARE, D), BF16),
        pltpu.VMEM((8, SHARE, D), BF16),
        pltpu.VMEM((SHARE, D), F32),
        pltpu.VMEM((TOK, D), BF16),
        pltpu.VMEM((TOK, WIDTH), F32),
        pltpu.VMEM((TOK, WIDTH), BF16),
        pltpu.VMEM((5, 2 * NLEN, WIDTH), BF16),
        pltpu.VMEM((5, 2 * NLEN, WIDTH), BF16),
    ]
    counts = (7, 4, 4, 4, 4, 8, 8, 4, 4, 4, 4, 8, 8, 8, 8, 8, 8, 8, 8, 2, 2)
    scratch += [pltpu.SemaphoreType.DMA((count,)) for count in counts]
    return pl.pallas_call(
        block_kernel,
        out_shape=jax.ShapeDtypeStruct((SHARE, D), F32),
        in_specs=[vmem] * 4 + [smem] * 2 + [hbm] * 7,
        out_specs=vmem,
        scratch_shapes=scratch,
        compiler_params=pltpu.CompilerParams(
            collective_id=0, has_side_effects=True, vmem_limit_bytes=56 << 20
        ),
        name="retro_block",
    )(
        query_rows,
        key_rows,
        value_rows,
        norm_gain.reshape(1, D),
        nb_shard,
        nb_row,
        hidden_in,
        w_self_out,
        w_cross_q,
        w_cross_k,
        w_cross_v,
        w_cross_out,
        enc_table,
    )


def solution(mesh):
    placed = (
        P("seq", None),
        P("seq", "db"),
        P("seq", "db"),
        P("seq", "db"),
        P("db", None),
        P(),
        P(None, "db"),
        P(None, "db"),
        P(None, "db"),
        P("db", None),
        P("db", None, None),
        P("seq", None),
        P("seq", None),
    )
    return jax.shard_map(
        per_device, mesh=mesh, in_specs=placed, out_specs=P(("seq", "db"), None), check_vma=False
    )
```

time: 420 us -> 185 us (0.44)
  waiting for transfers between devices: 358 us -> 0 us
  Pallas kernels: 0 us -> 178 us
  matrix products: 15.3 us -> 0 us
  between operations: 13.5 us -> 0.01 us
  other arithmetic: 10.3 us -> 0 us
  local copies, waits for them, and re-layouts: 14.5 us -> 5.87 us
  loops' own time: 5.49 us -> 0 us
    pallas_call x0 -> x1, Pallas kernels: none -> 178 us  [per_device(): pl.pallas_call(block_kernel, out_shape=jax.ShapeDtypeStruct((SHARE, D), F...]
    all_gather x3 -> x0, waiting for transfers between devices: 159 us -> none  [the longest x1 71.1 us: per_device(): arrived = lax.all_gather(outgoing, 'db', axis=0, tiled=True)]
    psum x1 -> x0, waiting for transfers between devices: 122 us -> none  [per_device(): lax.psum(jnp.dot(attended, w_self_out, preferred_element_type=jnp.float32...]
    reduce_scatter x1 -> x0, waiting for transfers between devices: 75.3 us -> none  [per_device(): lax.psum_scatter(jnp.dot(cross_mixed, w_cross_out, preferred_element_type...]
    dot_general x9 -> x0, matrix products: 15.3 us -> none  [the longest x1 4.8 us: per_device(): jnp.dot(attended, w_self_out, preferred_element_type=jnp.float32)]
    add x6 -> x0, other arithmetic: 7.17 us -> none  [the longest x1 5.18 us: per_device(): residual = hidden_in.astype(jnp.float32) + attn_total]
    another operation x9 -> x0, loops' own time: 5.49 us -> none  [the longest x1 5.29 us: fold_piece(): return lax.fori_loop(0, block_count, one_block, carried)]
  transfers between devices with their start and end apart: 6 -> 0, of which waited for: 6 -> 0; matrix products, arithmetic and copies ran while one was open for 3% -> 0% of each run, Pallas kernels for 0% -> 0%
where the time goes in v1:
time: 185 us; the launch traced here: 184 us
  Pallas kernels  178 us (96%)
  local copies, waits for them, and re-layouts  5.87 us (3%)
    pallas_call x1, Pallas kernels, per_device(): pl.pallas_call(block_kernel, out_shape=jax.ShapeDtypeStruct((SHARE, D), F...  178 us
    unnamed x3, local copies, waits for them, and re-layouts  4.56 us

profile of v1, /device:TPU:0, one launch (start us, length us, event | category | flops | bytes accessed | tf_op | source)
XLA Modules:
  0.0 183.9 jit_solution(4331248074674068512)
XLA Ops:
  0.0 1.4 copy.14.shard_ref
  1.4 1.3 copy.15.row_ref
  2.7 1.3 reshape.3.gain_ref
  4.0 178.0 %retro_block.1 = f32[32,4096]{1,0:T(8,128)} custom-call(bf16[256,512]{1,0:T(8,128)(2,1)} %q_ref.1, bf16[256,512]{1,0:T(8,128)(2,1)} %k_ref.1, bf16[256,512]{1,0:T(8,128)(2,1)} %v_ref.1, bf16[1,4096]{1,0:T(2,128)(2,1)} %reshape.3.gain_ref, s32[4,2]{1,0:T(4,128)} %copy.14.shard_ref, s32[4,2]{1,0:T(4,128)} %copy.15.row_ref, bf16[256,4096]{1,0:T(8,128)(2,1)} %hidden_hbm.1, ...), custom_call_target="tpu_custom_call" | custom-call | tf_op jit(solution)/shard_map/retro_block/pallas_call | solution.py:468
  182.0 1.9 %copy.17 = f32[32,4096]{1,0:T(8,128)} copy(f32[32,4096]{1,0:T(8,128)} %retro_block.1) | data formatting | bytes 1048576

commit v2 on v1

--- a/solution.py
+++ b/solution.py
@@ -1,4 +1,3 @@
-import functools
 import math
 
 import jax
@@ -15,6 +14,7 @@
 WIDTH = 512
 D = 4096
 SHARE = 32
+HALF = 2048
 NEG_BIG = -1e30
 MESH = pl.DeviceIdType.MESH
 EXP2_SCALE = math.log2(math.e) / math.sqrt(HD)
@@ -68,13 +68,22 @@
     lsum,
     acc,
     att,
-    enc_out,
     arr,
-    part,
-    rs1,
-    rs2,
+    part_a,
+    part_b,
+    za1,
+    ya1,
+    yb1,
+    zb1,
+    za2,
+    ya2,
+    yb2,
+    zb2,
+    sum_a,
+    sum_b,
     res,
-    nf,
+    nf_a,
+    nf_b,
     cqa,
     qx,
     kx,
@@ -106,6 +115,10 @@
     c = s % 2
     x = (s // 2) % 4
     zl = s // 8
+    y = d // 2
+    zh = d % 2
+    over = 2 * y + 1 - zh
+    far = (2, 1, 3)
 
     def at(zz, xx, cc):
         return (zz * 4 + xx) * 2 + cc
@@ -161,6 +174,41 @@
         def _():
             pltpu.make_async_copy(qst.at[h], qb.at[slot_to], qr.at[slot_to]).start()
 
+    def gather_start_y(piece_b, send, recv):
+        for dy in far:
+            peer = 2 * ((y + dy) % 4) + zh
+            start(remote(piece_b(d), piece_b(d), send.at[dy], recv.at[dy], s, peer))
+
+    def gather_start_z(piece_a, piece_b, send, recv):
+        start(remote(piece_a(d), piece_a(d), send.at[0], recv.at[0], s, over))
+        start(remote(piece_b(d), piece_b(d), send.at[12], recv.at[12], s, over))
+        for dy in far:
+            peer = 2 * ((y + dy) % 4) + zh
+            start(remote(piece_a(d), piece_a(d), send.at[4 + dy], recv.at[4 + dy], s, peer))
+
+    def gather_forward(piece_a, piece_b, send, recv):
+        remote(piece_a(over), piece_a(over), send.at[0], recv.at[0], s, over).wait_recv()
+        for dy in far:
+            peer = 2 * ((y + dy) % 4) + zh
+            start(remote(piece_a(over), piece_a(over), send.at[8 + dy], recv.at[8 + dy], s, peer))
+        for dy in (1, 3, 2):
+            src = 2 * ((y - dy + 4) % 4) + zh
+            remote(piece_b(src), piece_b(src), send.at[dy], recv.at[dy], s, src).wait_recv()
+            start(
+                remote(piece_b(src), piece_b(src), send.at[12 + dy], recv.at[12 + dy], s, over)
+            )
+
+    def gather_finish(piece_a, piece_b, send, recv):
+        for dy in (1, 3, 2):
+            src = 2 * ((y - dy + 4) % 4) + zh
+            remote(piece_a(src), piece_a(src), send.at[4 + dy], recv.at[4 + dy], s, src).wait_recv()
+        for dy in (1, 3, 2):
+            src = 2 * ((y - dy + 4) % 4) + 1 - zh
+            remote(piece_a(src), piece_a(src), send.at[8 + dy], recv.at[8 + dy], s, src).wait_recv()
+        for dy in (0, 1, 3, 2):
+            src = 2 * ((y - dy + 4) % 4) + 1 - zh
+            remote(piece_b(src), piece_b(src), send.at[12 + dy], recv.at[12 + dy], s, over).wait_recv()
+
     loads[0].wait()
     first = jnp.int32(0)
     second = jnp.int32(0)
@@ -171,8 +219,11 @@
         first = jnp.where(match & (found == 0), row, first)
         second = jnp.where(match & (found == 1), row, second)
         found = found + match.astype(jnp.int32)
-    enc_out[0] = enc[first]
-    enc_out[1] = enc[second]
+    arr[d] = enc[first]
+    arr[8 + d] = enc[second]
+    enc_a = lambda i: arr.at[i]
+    enc_b = lambda i: arr.at[8 + i]
+    gather_start_y(enc_b, es, er)
 
     def forward(src, k):
         start(remote(kv.at[src], kv.at[src], zs.at[k], zr.at[k], at(1 - zl, x, c), d))
@@ -183,12 +234,7 @@
         src = at(zl, (x - dx + 4) % 4, c)
         remote(kv.at[src], kv.at[src], xs.at[dx], xr.at[dx], src, d).wait_recv()
         forward(src, dx)
-    for dd in (1, 7, 2, 6, 3, 5, 4):
-        start(
-            remote(enc_out, arr.at[pl.ds(2 * d, 2)], es.at[dd], er.at[dd], s, (d + dd) % 8)
-        )
-    arr[2 * d] = enc_out[0]
-    arr[2 * d + 1] = enc_out[1]
+    gather_start_z(enc_a, enc_b, es, er)
     for dx in (0, 1, 3, 2):
         src = at(1 - zl, (x - dx + 4) % 4, c)
         remote(kv.at[src], kv.at[src], zs.at[dx], zr.at[dx], src, d).wait_recv()
@@ -198,6 +244,8 @@
             src = at((zl + zz) % 2, (x - dx + 4) % 4, 1 - c)
             k = 4 * zz + dx
             remote(kv.at[src], kv.at[src], cs.at[k], cr.at[k], src, d).wait_recv()
+
+    gather_forward(enc_a, enc_b, es, er)
 
     j = zl * 2 + c
 
@@ -264,35 +312,127 @@
     def project(lhs, weight):
         def tile(n, carry):
             cols = pl.ds(pl.multiple_of(n * 512, 512), 512)
-            part[:, cols] = dot_f32(lhs, weight[:, cols]).astype(BF16)
+            right = pl.ds(pl.multiple_of(HALF + n * 512, 512), 512)
+            product = dot_f32(lhs, weight[:, cols]).astype(BF16)
+            for share in range(8):
+                part_a[(share % 2) * 4 + share // 2, :, cols] = product[
+                    share * SHARE : (share + 1) * SHARE
+                ]
+            product = dot_f32(lhs, weight[:, right]).astype(BF16)
+            part_b[:, :, cols] = product.reshape(8, SHARE, 512)
             return carry
 
-        lax.fori_loop(0, 8, tile, 0)
+        lax.fori_loop(0, 4, tile, 0)
+
+    spread = []
+
+    def go(copy):
+        copy.start()
+        spread.append(copy)
+
+    def scatter(send, recv, za, ya, yb, zb):
+        for dy in (2, 1, 3, 0):
+            yy = (y + dy) % 4
+            go(
+                remote(
+                    part_a.at[(1 - zh) * 4 + yy], za.at[yy], send.at[dy], recv.at[dy], s, over
+                )
+            )
+            if dy:
+                go(
+                    remote(
+                        part_b.at[pl.ds(2 * yy, 2)],
+                        yb.at[dy],
+                        send.at[4 + dy],
+                        recv.at[4 + dy],
+                        s,
+                        2 * yy + zh,
+                    )
+                )
+        for dy in far:
+            yy = (y + dy) % 4
+            remote(za.at[yy], za.at[yy], send.at[dy], recv.at[dy], s, over).wait_recv()
+            sum_a[dy] = (part_a[zh * 4 + yy].astype(F32) + za[yy].astype(F32)).astype(BF16)
+            go(
+                remote(
+                    sum_a.at[dy], ya.at[dy], send.at[8 + dy], recv.at[8 + dy], s, 2 * yy + zh
+                )
+            )
+        for dy in far:
+            remote(yb.at[dy], yb.at[dy], send.at[4 + dy], recv.at[4 + dy], s, d).wait_recv()
+        total = part_b[over].astype(F32)
+        for dy in range(1, 4):
+            total = total + yb[dy, 1 - zh].astype(F32)
+        sum_b[...] = total.astype(BF16)
+        go(remote(sum_b, zb, send.at[12], recv.at[12], s, over))
+
+    def scatter_wait(send, recv, za, ya, zb):
+        remote(za.at[0], za.at[y], send.at[0], recv.at[0], s, over).wait_recv()
+        for dy in far:
+            remote(ya.at[dy], ya.at[dy], send.at[8 + dy], recv.at[8 + dy], s, d).wait_recv()
+        remote(zb, zb, send.at[12], recv.at[12], s, over).wait_recv()
+
+    def total_of(half, cols, za, ya, yb, zb):
+        if half == 0:
+            total = part_a[zh * 4 + y, :, cols].astype(F32) + za[y, :, cols].astype(F32)
+            for dy in range(1, 4):
+                total = total + ya[dy, :, cols].astype(F32)
+        else:
+            total = part_b[d, :, cols].astype(F32) + zb[:, cols].astype(F32)
+            for dy in range(1, 4):
+                total = total + yb[dy, zh, :, cols].astype(F32)
+        return total
 
     loads[1].wait()
     project(att[...], wso)
-    spread = []
-    for dd in (4, 3, 5, 2, 6, 1, 7):
-        other = (d + dd) % 8
-        rows = pl.ds(pl.multiple_of(other * SHARE, SHARE), SHARE)
-        copy = remote(part.at[rows], rs1.at[dd], r1s.at[dd], r1r.at[dd], s, other)
-        copy.start()
-        spread.append(copy)
-
-    for dd in range(1, 8):
-        src = (d - dd + 8) % 8
-        remote(enc_out, arr.at[pl.ds(2 * src, 2)], es.at[dd], er.at[dd], s, src).wait_recv()
+    scatter(r1s, r1r, za1, ya1, yb1, zb1)
+
+    loads[2].wait()
+    scatter_wait(r1s, r1r, za1, ya1, zb1)
+
+    def add_up(n, square):
+        cols = pl.ds(pl.multiple_of(n * 512, 512), 512)
+        for half in range(2):
+            wide = pl.ds(pl.multiple_of(half * HALF + n * 512, 512), 512)
+            total = total_of(half, cols, za1, ya1, yb1, zb1) + hid[:, wide].astype(F32)
+            res[:, wide] = total
+            square = square + total * total
+        return square
+
+    square = lax.fori_loop(0, 4, add_up, jnp.zeros((SHARE, 512), F32))
+    scale = lax.rsqrt(jnp.sum(square, axis=-1, keepdims=True) / D + 1e-05)
+
+    def normalise(n, carry):
+        cols = pl.ds(pl.multiple_of(n * 512, 512), 512)
+        for half, held in enumerate((nf_a, nf_b)):
+            wide = pl.ds(pl.multiple_of(half * HALF + n * 512, 512), 512)
+            held[d, :, cols] = (
+                res[:, wide] * scale * gain_ref[:, wide].astype(F32)
+            ).astype(BF16)
+        return carry
+
+    lax.fori_loop(0, 4, normalise, 0)
+    share_a = lambda i: nf_a.at[i]
+    share_b = lambda i: nf_b.at[i]
+    gather_start_y(share_b, ags, agr)
+    gather_start_z(share_a, share_b, ags, agr)
+
+    gather_finish(enc_a, enc_b, es, er)
     loads[3].wait()
     loads[4].wait()
-    for e in range(8):
+
+    def cross_pair(e):
         shard = shard_ref[e // 2, e % 2]
         rank = jnp.int32(0)
         for earlier in range(e):
             rank = rank + (shard_ref[earlier // 2, earlier % 2] == shard).astype(jnp.int32)
-        entry = arr[shard * 2 + rank]
+        entry = arr[jnp.minimum(rank, 1) * 8 + shard]
         rows = slice((e % 2) * NLEN, (e % 2 + 1) * NLEN)
         kx[e // 2 + 1, rows, :] = dot_f32(entry, wck[...]).astype(BF16)
         vx[e // 2 + 1, rows, :] = dot_f32(entry, wcv[...]).astype(BF16)
+
+    cross_pair(6)
+    cross_pair(7)
 
     @pl.when(s < 15)
     def _():
@@ -304,48 +444,26 @@
         kx[0] = jnp.zeros((2 * NLEN, WIDTH), BF16)
         vx[0] = jnp.zeros((2 * NLEN, WIDTH), BF16)
 
-    loads[2].wait()
-    for dd in range(1, 8):
-        remote(part.at[own_rows], rs1.at[dd], r1s.at[dd], r1r.at[dd], s, d).wait_recv()
-
-    def add_up(n, square):
-        cols = pl.ds(pl.multiple_of(n * 512, 512), 512)
-        total = part[own_rows, cols].astype(F32)
-        for dd in range(1, 8):
-            total = total + rs1[dd, :, cols].astype(F32)
-        total = total + hid[:, cols].astype(F32)
-        res[:, cols] = total
-        return square + total * total
-
-    square = lax.fori_loop(0, 8, add_up, jnp.zeros((SHARE, 512), F32))
-    scale = lax.rsqrt(jnp.sum(square, axis=-1, keepdims=True) / D + 1e-05)
-
-    def normalise(n, carry):
-        cols = pl.ds(pl.multiple_of(n * 512, 512), 512)
-        nf[own_rows, cols] = (res[:, cols] * scale * gain_ref[:, cols].astype(F32)).astype(BF16)
-        return carry
-
-    lax.fori_loop(0, 8, normalise, 0)
-    for dd in (4, 3, 5, 2, 6, 1, 7):
-        start(
-            remote(nf.at[own_rows], nf.at[own_rows], ags.at[dd], agr.at[dd], s, (d + dd) % 8)
-        )
+    gather_forward(share_a, share_b, ags, agr)
+    for e in range(6):
+        cross_pair(e)
     for copy in spread:
         copy.wait_send()
+    spread.clear()
     loads[5].wait()
-    for dd in range(1, 8):
-        src = (d - dd + 8) % 8
-        rows = pl.ds(pl.multiple_of(src * SHARE, SHARE), SHARE)
-        remote(nf.at[rows], nf.at[rows], ags.at[dd], agr.at[dd], s, src).wait_recv()
+    gather_finish(share_a, share_b, ags, agr)
 
     cqa[...] = jnp.zeros_like(cqa)
 
     def contract(n, carry):
         cols = pl.ds(pl.multiple_of(n * 512, 512), 512)
-        cqa[...] += dot_f32(nf[:, cols], wcq[cols, :])
+        right = pl.ds(pl.multiple_of(HALF + n * 512, 512), 512)
+        cqa[...] += dot_f32(nf_a[:, :, cols].reshape(TOK, 512), wcq[cols, :]) + dot_f32(
+            nf_b[:, :, cols].reshape(TOK, 512), wcq[right, :]
+        )
         return carry
 
-    lax.fori_loop(0, 8, contract, 0)
+    lax.fori_loop(0, 4, contract, 0)
     qx[...] = pltpu.roll(cqa[...].astype(BF16).astype(F32), 1, 0).astype(BF16)
 
     @pl.when(s > 0)
@@ -377,23 +495,20 @@
 
     loads[6].wait()
     project(att[...], wco)
-    for dd in (4, 3, 5, 2, 6, 1, 7):
-        other = (d + dd) % 8
-        rows = pl.ds(pl.multiple_of(other * SHARE, SHARE), SHARE)
-        start(remote(part.at[rows], rs2.at[dd], r2s.at[dd], r2r.at[dd], s, other))
-    for dd in range(1, 8):
-        remote(part.at[own_rows], rs2.at[dd], r2s.at[dd], r2r.at[dd], s, d).wait_recv()
+    scatter(r2s, r2r, za2, ya2, yb2, zb2)
+    scatter_wait(r2s, r2r, za2, ya2, zb2)
 
     def finish(n, carry):
         cols = pl.ds(pl.multiple_of(n * 512, 512), 512)
-        total = part[own_rows, cols].astype(F32)
-        for dd in range(1, 8):
-            total = total + rs2[dd, :, cols].astype(F32)
-        out_ref[:, cols] = res[:, cols] + total
+        for half in range(2):
+            wide = pl.ds(pl.multiple_of(half * HALF + n * 512, 512), 512)
+            out_ref[:, wide] = res[:, wide] + total_of(half, cols, za2, ya2, yb2, zb2)
         return carry
 
-    lax.fori_loop(0, 8, finish, 0)
-
+    lax.fori_loop(0, 4, finish, 0)
+
+    for copy in spread:
+        copy.wait_send()
     for copy in sends:
         copy.wait_send()
     for h in range(4):
@@ -451,19 +566,28 @@
         pltpu.VMEM((TOK, HD), F32),
         pltpu.VMEM((TOK, HD), F32),
         pltpu.VMEM((TOK, WIDTH), BF16),
-        pltpu.VMEM((2, NLEN, 1024), BF16),
         pltpu.VMEM((16, NLEN, 1024), BF16),
-        pltpu.VMEM((TOK, D), BF16),
-        pltpu.VMEM((8, SHARE, D), BF16),
-        pltpu.VMEM((8, SHARE, D), BF16),
+        pltpu.VMEM((8, SHARE, HALF), BF16),
+        pltpu.VMEM((8, SHARE, HALF), BF16),
+    ]
+    scratch += [
+        pltpu.VMEM((4, SHARE, HALF), BF16),
+        pltpu.VMEM((4, SHARE, HALF), BF16),
+        pltpu.VMEM((4, 2, SHARE, HALF), BF16),
+        pltpu.VMEM((SHARE, HALF), BF16),
+    ] * 2
+    scratch += [
+        pltpu.VMEM((4, SHARE, HALF), BF16),
+        pltpu.VMEM((SHARE, HALF), BF16),
         pltpu.VMEM((SHARE, D), F32),
-        pltpu.VMEM((TOK, D), BF16),
+        pltpu.VMEM((8, SHARE, HALF), BF16),
+        pltpu.VMEM((8, SHARE, HALF), BF16),
         pltpu.VMEM((TOK, WIDTH), F32),
         pltpu.VMEM((TOK, WIDTH), BF16),
         pltpu.VMEM((5, 2 * NLEN, WIDTH), BF16),
         pltpu.VMEM((5, 2 * NLEN, WIDTH), BF16),
     ]
-    counts = (7, 4, 4, 4, 4, 8, 8, 4, 4, 4, 4, 8, 8, 8, 8, 8, 8, 8, 8, 2, 2)
+    counts = (7, 4, 4, 4, 4, 8, 8, 4, 4, 4, 4, 16, 16, 13, 13, 16, 16, 13, 13, 2, 2)
     scratch += [pltpu.SemaphoreType.DMA((count,)) for count in counts]
     return pl.pallas_call(
         block_kernel,

time: 185 us -> 135 us (0.73)
  the two profiles are of different devices: /device:TPU:0 before, /device:TPU:4 now
where the time goes in v2:
time: 135 us
  Pallas kernels  129 us (96%)
  local copies, waits for them, and re-layouts  5.87 us (4%)
    pallas_call x1, Pallas kernels, per_device(): pl.pallas_call(block_kernel, out_shape=jax.ShapeDtypeStruct((SHARE, D), F...  129 us
    unnamed x3, local copies, waits for them, and re-layouts  4.56 us

profile of v2, /device:TPU:4, one launch (start us, length us, event | category | flops | bytes accessed | tf_op | source)
XLA Modules:
  0.0 135.2 jit_solution(3474240651647032821)
XLA Ops:
  0.0 1.4 copy.14.shard_ref
  1.4 1.3 copy.15.row_ref
  2.7 1.3 reshape.3.gain_ref
  4.0 129.3 %retro_block.1 = f32[32,4096]{1,0:T(8,128)} custom-call(bf16[256,512]{1,0:T(8,128)(2,1)} %q_ref.1, bf16[256,512]{1,0:T(8,128)(2,1)} %k_ref.1, bf16[256,512]{1,0:T(8,128)(2,1)} %v_ref.1, bf16[1,4096]{1,0:T(2,128)(2,1)} %reshape.3.gain_ref, s32[4,2]{1,0:T(4,128)} %copy.14.shard_ref, s32[4,2]{1,0:T(4,128)} %copy.15.row_ref, bf16[256,4096]{1,0:T(8,128)(2,1)} %hidden_hbm.1, ...), custom_call_target="tpu_custom_call" | custom-call | tf_op jit(solution)/shard_map/retro_block/pallas_call | solution.py:592
  133.3 1.9 %copy.17 = f32[32,4096]{1,0:T(8,128)} copy(f32[32,4096]{1,0:T(8,128)} %retro_block.1) | data formatting | bytes 1048576

commit v3 on v2

--- a/solution.py
+++ b/solution.py
@@ -40,9 +40,9 @@
     q_ref,
     k_ref,
     v_ref,
-    gain_ref,
-    shard_ref,
-    row_ref,
+    gain_hbm,
+    shard_hbm,
+    row_hbm,
     hidden_hbm,
     wso_hbm,
     wcq_hbm,
@@ -51,6 +51,9 @@
     wco_hbm,
     enc_hbm,
     out_ref,
+    gain,
+    shard_ref,
+    row_ref,
     wso,
     wcq,
     wck,
@@ -81,6 +84,7 @@
     zb2,
     sum_a,
     sum_b,
+    sum_y,
     res,
     nf_a,
     nf_b,
@@ -139,9 +143,12 @@
         pltpu.make_async_copy(wcv_hbm, wcv, wsem.at[4]),
         pltpu.make_async_copy(wcq_hbm, wcq, wsem.at[5]),
         pltpu.make_async_copy(wco_hbm, wco, wsem.at[6]),
+        pltpu.make_async_copy(shard_hbm, shard_ref, wsem.at[7]),
+        pltpu.make_async_copy(row_hbm, row_ref, wsem.at[8]),
+        pltpu.make_async_copy(gain_hbm, gain, wsem.at[9]),
     ]
-    for load in loads:
-        load.start()
+    for k in (0, 7, 8):
+        loads[k].start()
     for h in range(4):
         cols = slice(h * HD, (h + 1) * HD)
         kvs[h, 0] = k_ref[:, cols]
@@ -159,6 +166,11 @@
         other = (x + dx) % 4
         start(remote(kvs.at[other], kv.at[s], xs.at[dx], xr.at[dx], at(zl, other, c), d))
     kv[s] = kvs[x]
+    def forward(src, k):
+        start(remote(kv.at[src], kv.at[src], zs.at[k], zr.at[k], at(1 - zl, x, c), d))
+        start(remote(kv.at[src], kv.at[src], cs.at[k], cr.at[k], at(zl, x, 1 - c), d))
+
+    forward(s, 0)
     low = s % 8
     high = low // 4
     j_to = (1 - high) * low + high * (7 - low)
@@ -174,67 +186,107 @@
         def _():
             pltpu.make_async_copy(qst.at[h], qb.at[slot_to], qr.at[slot_to]).start()
 
-    def gather_start_y(piece_b, send, recv):
-        for dy in far:
-            peer = 2 * ((y + dy) % 4) + zh
-            start(remote(piece_b(d), piece_b(d), send.at[dy], recv.at[dy], s, peer))
-
-    def gather_start_z(piece_a, piece_b, send, recv):
-        start(remote(piece_a(d), piece_a(d), send.at[0], recv.at[0], s, over))
-        start(remote(piece_b(d), piece_b(d), send.at[12], recv.at[12], s, over))
-        for dy in far:
-            peer = 2 * ((y + dy) % 4) + zh
-            start(remote(piece_a(d), piece_a(d), send.at[4 + dy], recv.at[4 + dy], s, peer))
-
-    def gather_forward(piece_a, piece_b, send, recv):
-        remote(piece_a(over), piece_a(over), send.at[0], recv.at[0], s, over).wait_recv()
-        for dy in far:
-            peer = 2 * ((y + dy) % 4) + zh
-            start(remote(piece_a(over), piece_a(over), send.at[8 + dy], recv.at[8 + dy], s, peer))
-        for dy in (1, 3, 2):
-            src = 2 * ((y - dy + 4) % 4) + zh
-            remote(piece_b(src), piece_b(src), send.at[dy], recv.at[dy], s, src).wait_recv()
-            start(
-                remote(piece_b(src), piece_b(src), send.at[12 + dy], recv.at[12 + dy], s, over)
-            )
-
-    def gather_finish(piece_a, piece_b, send, recv):
-        for dy in (1, 3, 2):
-            src = 2 * ((y - dy + 4) % 4) + zh
-            remote(piece_a(src), piece_a(src), send.at[4 + dy], recv.at[4 + dy], s, src).wait_recv()
-        for dy in (1, 3, 2):
-            src = 2 * ((y - dy + 4) % 4) + 1 - zh
-            remote(piece_a(src), piece_a(src), send.at[8 + dy], recv.at[8 + dy], s, src).wait_recv()
-        for dy in (0, 1, 3, 2):
-            src = 2 * ((y - dy + 4) % 4) + 1 - zh
-            remote(piece_b(src), piece_b(src), send.at[12 + dy], recv.at[12 + dy], s, over).wait_recv()
-
-    loads[0].wait()
+    def share_at(step, side):
+        return 2 * ((y + step + 4) % 4) + side
+
+    def flow_copies(flow, piece, side, sems):
+        send, recv = sems
+        held = piece(share_at(0, side), 0)
+        return [
+            remote(held, held, send.at[4 * flow + k], recv.at[4 * flow + k], s, share_at(step, zh))
+            for k, step in ((0, 1), (1, -1))
+        ]
+
+    def flow_send(flow, piece, side, sems):
+        for copy in flow_copies(flow, piece, side, sems):
+            start(copy)
+
+    def flow_forward(flow, piece, side, sems, then=None):
+        send, recv = sems
+        for k, step in ((0, 1), (1, -1)):
+            came = share_at(-step, side)
+            held = piece(came, 0)
+            remote(held, held, send.at[4 * flow + k], recv.at[4 * flow + k], s, d).wait_recv()
+            part = piece(came, 1 + k)
+            k2 = 4 * flow + 2 + k
+            start(remote(part, part, send.at[k2], recv.at[k2], s, share_at(step, zh)))
+            if then is not None:
+                then(came, k)
+
+    def flow_last(flow, piece, side, sems):
+        send, recv = sems
+        for k in range(2):
+            part = piece(share_at(2, side), 1 + k)
+            k2 = 4 * flow + 2 + k
+            remote(part, part, send.at[k2], recv.at[k2], s, d).wait_recv()
+
+    def cross_send(piece, owner, k, sems):
+        send, recv = sems
+        held = piece(owner, 0)
+        start(remote(held, held, send.at[k], recv.at[k], s, over))
+
+    def cross_wait(piece, owner, k, sems):
+        send, recv = sems
+        held = piece(owner, 0)
+        remote(held, held, send.at[k], recv.at[k], s, over).wait_recv()
+
+    def gather_b_on(piece_b, sems):
+        flow_forward(2, piece_b, zh, sems, lambda came, k: cross_send(piece_b, came, 14 + k, sems))
+
+    def gather_a_over(piece_a, sems):
+        cross_wait(piece_a, over, 12, sems)
+        for copy in flow_copies(1, piece_a, 1 - zh, sems):
+            copy.start()
+
+    def gather_a_sent(piece_a, sems):
+        for copy in flow_copies(1, piece_a, 1 - zh, sems):
+            copy.wait_send()
+
+    def gather_last_on(piece_a, piece_b, sems):
+        flow_last(2, piece_b, zh, sems)
+        cross_send(piece_b, share_at(2, zh), 16, sems)
+        flow_forward(1, piece_a, 1 - zh, sems)
+
+    def gather_finish_a(piece_a, sems):
+        flow_last(0, piece_a, zh, sems)
+        flow_last(1, piece_a, 1 - zh, sems)
+
+    def gather_finish_b(piece_b, sems):
+        for k, step in ((13, 0), (14, -1), (15, 1), (16, 2)):
+            cross_wait(piece_b, share_at(step, 1 - zh), k, sems)
+
+    for k in (0, 7, 8):
+        loads[k].wait()
+    for k in (1, 2, 3, 4, 5, 6, 9):
+        loads[k].start()
     first = jnp.int32(0)
     second = jnp.int32(0)
     found = jnp.int32(0)
     for e in range(8):
-        match = shard_ref[e // 2, e % 2] == d
-        row = row_ref[e // 2, e % 2]
+        match = shard_ref[e % 2, e // 2] == d
+        row = row_ref[e % 2, e // 2]
         first = jnp.where(match & (found == 0), row, first)
         second = jnp.where(match & (found == 1), row, second)
         found = found + match.astype(jnp.int32)
-    arr[d] = enc[first]
-    arr[8 + d] = enc[second]
-    enc_a = lambda i: arr.at[i]
-    enc_b = lambda i: arr.at[8 + i]
-    gather_start_y(enc_b, es, er)
-
-    def forward(src, k):
-        start(remote(kv.at[src], kv.at[src], zs.at[k], zr.at[k], at(1 - zl, x, c), d))
-        start(remote(kv.at[src], kv.at[src], cs.at[k], cr.at[k], at(zl, x, 1 - c), d))
-
-    forward(s, 0)
+    arr[d, 0:NLEN] = enc[first]
+    arr[d, NLEN : 2 * NLEN] = enc[second]
+
+    def enc_a(i, part):
+        return arr.at[i, pl.ds((0, 0, 96)[part], (192, 96, 96)[part])]
+
+    def enc_b(i, part):
+        return arr.at[i, pl.ds((192, 192, 224)[part], (64, 32, 32)[part])]
+
+    enc_sems = (es, er)
+    cross_send(enc_a, d, 12, enc_sems)
+    flow_send(2, enc_b, zh, enc_sems)
+    flow_send(0, enc_a, zh, enc_sems)
+
     for dx in (1, 3, 2):
         src = at(zl, (x - dx + 4) % 4, c)
         remote(kv.at[src], kv.at[src], xs.at[dx], xr.at[dx], src, d).wait_recv()
         forward(src, dx)
-    gather_start_z(enc_a, enc_b, es, er)
+    cross_send(enc_b, d, 13, enc_sems)
     for dx in (0, 1, 3, 2):
         src = at(1 - zl, (x - dx + 4) % 4, c)
         remote(kv.at[src], kv.at[src], zs.at[dx], zr.at[dx], src, d).wait_recv()
@@ -245,7 +297,9 @@
             k = 4 * zz + dx
             remote(kv.at[src], kv.at[src], cs.at[k], cr.at[k], src, d).wait_recv()
 
-    gather_forward(enc_a, enc_b, es, er)
+    gather_a_over(enc_a, enc_sems)
+    gather_b_on(enc_b, enc_sems)
+    flow_forward(0, enc_a, zh, enc_sems)
 
     j = zl * 2 + c
 
@@ -254,6 +308,7 @@
 
     def slot(i, carry):
         b = block_of(i)
+
         remote(qst.at[0], qb.at[i], qs.at[0], qr.at[i], s, d).wait_recv()
         query = qb[i]
         last = (b + 2) // 2 - 1
@@ -305,19 +360,27 @@
         return carry
 
     lax.fori_loop(0, 4, slot, 0)
+    gather_last_on(enc_a, enc_b, enc_sems)
     for h in range(4):
         remote(ob.at[0], ret.at[h], os_.at[0], or_.at[h], s, d).wait_recv()
         att[:, h * HD : (h + 1) * HD] = ret[h]
 
-    def project(lhs, weight):
+    def project_a(lhs, weight):
         def tile(n, carry):
             cols = pl.ds(pl.multiple_of(n * 512, 512), 512)
-            right = pl.ds(pl.multiple_of(HALF + n * 512, 512), 512)
             product = dot_f32(lhs, weight[:, cols]).astype(BF16)
             for share in range(8):
                 part_a[(share % 2) * 4 + share // 2, :, cols] = product[
                     share * SHARE : (share + 1) * SHARE
                 ]
+            return carry
+
+        lax.fori_loop(0, 4, tile, 0)
+
+    def project_b(lhs, weight):
+        def tile(n, carry):
+            cols = pl.ds(pl.multiple_of(n * 512, 512), 512)
+            right = pl.ds(pl.multiple_of(HALF + n * 512, 512), 512)
             product = dot_f32(lhs, weight[:, right]).astype(BF16)
             part_b[:, :, cols] = product.reshape(8, SHARE, 512)
             return carry
@@ -330,25 +393,43 @@
         copy.start()
         spread.append(copy)
 
-    def scatter(send, recv, za, ya, yb, zb):
+    def scatter(lhs, weight, send, recv, za, ya, yb, zb):
+        project_a(lhs, weight)
         for dy in (2, 1, 3, 0):
             yy = (y + dy) % 4
+            go(remote(part_a.at[(1 - zh) * 4 + yy], za.at[yy], send.at[dy], recv.at[dy], s, over))
+        project_b(lhs, weight)
+        steps = ((0, 1), (1, -1))
+        for k, step in steps:
             go(
                 remote(
-                    part_a.at[(1 - zh) * 4 + yy], za.at[yy], send.at[dy], recv.at[dy], s, over
+                    part_b.at[share_at(2, k)],
+                    yb.at[k],
+                    send.at[4 + k],
+                    recv.at[4 + k],
+                    s,
+                    share_at(step, zh),
                 )
             )
-            if dy:
-                go(
-                    remote(
-                        part_b.at[pl.ds(2 * yy, 2)],
-                        yb.at[dy],
-                        send.at[4 + dy],
-                        recv.at[4 + dy],
-                        s,
-                        2 * yy + zh,
-                    )
+        for k, step in steps:
+            go(
+                remote(
+                    part_b.at[share_at(step, 1 - k)],
+                    yb.at[4 + k],
+                    send.at[12 + k],
+                    recv.at[12 + k],
+                    s,
+                    share_at(step, zh),
                 )
+            )
+        for k, step in steps:
+            remote(yb.at[k], yb.at[k], send.at[4 + k], recv.at[4 + k], s, d).wait_recv()
+            sum_y[k] = (part_b[share_at(step, k)].astype(F32) + yb[k].astype(F32)).astype(BF16)
+            go(
+                remote(
+                    sum_y.at[k], yb.at[2 + k], send.at[6 + k], recv.at[6 + k], s, share_at(step, zh)
+                )
+            )
         for dy in far:
             yy = (y + dy) % 4
             remote(za.at[yy], za.at[yy], send.at[dy], recv.at[dy], s, over).wait_recv()
@@ -358,19 +439,24 @@
                     sum_a.at[dy], ya.at[dy], send.at[8 + dy], recv.at[8 + dy], s, 2 * yy + zh
                 )
             )
-        for dy in far:
-            remote(yb.at[dy], yb.at[dy], send.at[4 + dy], recv.at[4 + dy], s, d).wait_recv()
-        total = part_b[over].astype(F32)
-        for dy in range(1, 4):
-            total = total + yb[dy, 1 - zh].astype(F32)
-        sum_b[...] = total.astype(BF16)
-        go(remote(sum_b, zb, send.at[12], recv.at[12], s, over))
+        for k in range(2):
+            remote(yb.at[2 + k], yb.at[2 + k], send.at[6 + k], recv.at[6 + k], s, d).wait_recv()
+            remote(yb.at[4 + k], yb.at[4 + k], send.at[12 + k], recv.at[12 + k], s, d).wait_recv()
+        sum_b[...] = b_share(over, 1 - zh, slice(None), yb).astype(BF16)
+        go(remote(sum_b, zb, send.at[14], recv.at[14], s, over))
+
+    def b_share(share, k, cols, yb):
+        return (
+            part_b[share, :, cols].astype(F32)
+            + yb[2 + k, :, cols].astype(F32)
+            + yb[5 - k, :, cols].astype(F32)
+        )
 
     def scatter_wait(send, recv, za, ya, zb):
         remote(za.at[0], za.at[y], send.at[0], recv.at[0], s, over).wait_recv()
         for dy in far:
             remote(ya.at[dy], ya.at[dy], send.at[8 + dy], recv.at[8 + dy], s, d).wait_recv()
-        remote(zb, zb, send.at[12], recv.at[12], s, over).wait_recv()
+        remote(zb, zb, send.at[14], recv.at[14], s, over).wait_recv()
 
     def total_of(half, cols, za, ya, yb, zb):
         if half == 0:
@@ -378,16 +464,14 @@
             for dy in range(1, 4):
                 total = total + ya[dy, :, cols].astype(F32)
         else:
-            total = part_b[d, :, cols].astype(F32) + zb[:, cols].astype(F32)
-            for dy in range(1, 4):
-                total = total + yb[dy, zh, :, cols].astype(F32)
+            total = b_share(d, zh, cols, yb) + zb[:, cols].astype(F32)
         return total
 
     loads[1].wait()
-    project(att[...], wso)
-    scatter(r1s, r1r, za1, ya1, yb1, zb1)
+    scatter(att[...], wso, r1s, r1r, za1, ya1, yb1, zb1)
 
     loads[2].wait()
+    loads[9].wait()
     scatter_wait(r1s, r1r, za1, ya1, zb1)
 
     def add_up(n, square):
@@ -407,26 +491,35 @@
         for half, held in enumerate((nf_a, nf_b)):
             wide = pl.ds(pl.multiple_of(half * HALF + n * 512, 512), 512)
             held[d, :, cols] = (
-                res[:, wide] * scale * gain_ref[:, wide].astype(F32)
+                res[:, wide] * scale * gain[wide].astype(F32)
             ).astype(BF16)
         return carry
 
     lax.fori_loop(0, 4, normalise, 0)
-    share_a = lambda i: nf_a.at[i]
-    share_b = lambda i: nf_b.at[i]
-    gather_start_y(share_b, ags, agr)
-    gather_start_z(share_a, share_b, ags, agr)
-
-    gather_finish(enc_a, enc_b, es, er)
+
+    def share_a(i, part):
+        return nf_a.at[i, pl.ds((0, 0, 16)[part], (32, 16, 16)[part])]
+
+    def share_b(i, part):
+        return nf_b.at[i, pl.ds((0, 0, 16)[part], (32, 16, 16)[part])]
+
+    ag_sems = (ags, agr)
+    cross_send(share_a, d, 12, ag_sems)
+    flow_send(2, share_b, zh, ag_sems)
+    flow_send(0, share_a, zh, ag_sems)
+    cross_send(share_b, d, 13, ag_sems)
+
+    gather_finish_a(enc_a, enc_sems)
+    gather_finish_b(enc_b, enc_sems)
     loads[3].wait()
     loads[4].wait()
 
     def cross_pair(e):
-        shard = shard_ref[e // 2, e % 2]
+        shard = shard_ref[e % 2, e // 2]
         rank = jnp.int32(0)
         for earlier in range(e):
-            rank = rank + (shard_ref[earlier // 2, earlier % 2] == shard).astype(jnp.int32)
-        entry = arr[jnp.minimum(rank, 1) * 8 + shard]
+            rank = rank + (shard_ref[earlier % 2, earlier // 2] == shard).astype(jnp.int32)
+        entry = arr.reshape(16, NLEN, 1024)[shard * 2 + jnp.minimum(rank, 1)]
         rows = slice((e % 2) * NLEN, (e % 2 + 1) * NLEN)
         kx[e // 2 + 1, rows, :] = dot_f32(entry, wck[...]).astype(BF16)
         vx[e // 2 + 1, rows, :] = dot_f32(entry, wcv[...]).astype(BF16)
@@ -444,26 +537,36 @@
         kx[0] = jnp.zeros((2 * NLEN, WIDTH), BF16)
         vx[0] = jnp.zeros((2 * NLEN, WIDTH), BF16)
 
-    gather_forward(share_a, share_b, ags, agr)
-    for e in range(6):
+    gather_a_over(share_a, ag_sems)
+    gather_b_on(share_b, ag_sems)
+    flow_forward(0, share_a, zh, ag_sems)
+    for e in range(4):
+        cross_pair(e)
+    gather_last_on(share_a, share_b, ag_sems)
+    for e in range(4, 6):
         cross_pair(e)
     for copy in spread:
         copy.wait_send()
     spread.clear()
     loads[5].wait()
-    gather_finish(share_a, share_b, ags, agr)
+    gather_finish_a(share_a, ag_sems)
 
     cqa[...] = jnp.zeros_like(cqa)
 
-    def contract(n, carry):
+    def contract_a(n, carry):
+        cols = pl.ds(pl.multiple_of(n * 512, 512), 512)
+        cqa[...] += dot_f32(nf_a[:, :, cols].reshape(TOK, 512), wcq[cols, :])
+        return carry
+
+    def contract_b(n, carry):
         cols = pl.ds(pl.multiple_of(n * 512, 512), 512)
         right = pl.ds(pl.multiple_of(HALF + n * 512, 512), 512)
-        cqa[...] += dot_f32(nf_a[:, :, cols].reshape(TOK, 512), wcq[cols, :]) + dot_f32(
-            nf_b[:, :, cols].reshape(TOK, 512), wcq[right, :]
-        )
+        cqa[...] += dot_f32(nf_b[:, :, cols].reshape(TOK, 512), wcq[right, :])
         return carry
 
-    lax.fori_loop(0, 4, contract, 0)
+    lax.fori_loop(0, 4, contract_a, 0)
+    gather_finish_b(share_b, ag_sems)
+    lax.fori_loop(0, 4, contract_b, 0)
     qx[...] = pltpu.roll(cqa[...].astype(BF16).astype(F32), 1, 0).astype(BF16)
 
     @pl.when(s > 0)
@@ -494,8 +597,7 @@
     att[...] = pltpu.roll(cqa[...], TOK - 1, 0).astype(BF16)
 
     loads[6].wait()
-    project(att[...], wco)
-    scatter(r2s, r2r, za2, ya2, yb2, zb2)
+    scatter(att[...], wco, r2s, r2r, za2, ya2, yb2, zb2)
     scatter_wait(r2s, r2r, za2, ya2, zb2)
 
     def finish(n, carry):
@@ -511,6 +613,8 @@
         copy.wait_send()
     for copy in sends:
         copy.wait_send()
+    gather_a_sent(enc_a, enc_sems)
+    gather_a_sent(share_a, ag_sems)
     for h in range(4):
         goal = at(j_to // 2, h, j_to % 2)
 
@@ -546,9 +650,11 @@
     nb_row,
 ):
     vmem = pl.BlockSpec(memory_space=pltpu.VMEM)
-    smem = pl.BlockSpec(memory_space=pltpu.SMEM)
     hbm = pl.BlockSpec(memory_space=pl.ANY)
     scratch = [
+        pltpu.VMEM((D,), BF16),
+        pltpu.SMEM((2, 4), jnp.int32),
+        pltpu.SMEM((2, 4), jnp.int32),
         pltpu.VMEM((WIDTH, D), BF16),
         pltpu.VMEM((D, WIDTH), BF16),
         pltpu.VMEM((1024, WIDTH), BF16),
@@ -566,19 +672,20 @@
         pltpu.VMEM((TOK, HD), F32),
         pltpu.VMEM((TOK, HD), F32),
         pltpu.VMEM((TOK, WIDTH), BF16),
-        pltpu.VMEM((16, NLEN, 1024), BF16),
+        pltpu.VMEM((8, 2 * NLEN, 1024), BF16),
         pltpu.VMEM((8, SHARE, HALF), BF16),
         pltpu.VMEM((8, SHARE, HALF), BF16),
     ]
     scratch += [
         pltpu.VMEM((4, SHARE, HALF), BF16),
         pltpu.VMEM((4, SHARE, HALF), BF16),
-        pltpu.VMEM((4, 2, SHARE, HALF), BF16),
+        pltpu.VMEM((6, SHARE, HALF), BF16),
         pltpu.VMEM((SHARE, HALF), BF16),
     ] * 2
     scratch += [
         pltpu.VMEM((4, SHARE, HALF), BF16),
         pltpu.VMEM((SHARE, HALF), BF16),
+        pltpu.VMEM((2, SHARE, HALF), BF16),
         pltpu.VMEM((SHARE, D), F32),
         pltpu.VMEM((8, SHARE, HALF), BF16),
         pltpu.VMEM((8, SHARE, HALF), BF16),
@@ -587,12 +694,12 @@
         pltpu.VMEM((5, 2 * NLEN, WIDTH), BF16),
         pltpu.VMEM((5, 2 * NLEN, WIDTH), BF16),
     ]
-    counts = (7, 4, 4, 4, 4, 8, 8, 4, 4, 4, 4, 16, 16, 13, 13, 16, 16, 13, 13, 2, 2)
+    counts = (10, 4, 4, 4, 4, 8, 8, 4, 4, 4, 4, 17, 17, 15, 15, 17, 17, 15, 15, 2, 2)
     scratch += [pltpu.SemaphoreType.DMA((count,)) for count in counts]
     return pl.pallas_call(
         block_kernel,
         out_shape=jax.ShapeDtypeStruct((SHARE, D), F32),
-        in_specs=[vmem] * 4 + [smem] * 2 + [hbm] * 7,
+        in_specs=[vmem] * 3 + [hbm] * 10,
         out_specs=vmem,
         scratch_shapes=scratch,
         compiler_params=pltpu.CompilerParams(
@@ -603,9 +710,9 @@
         query_rows,
         key_rows,
         value_rows,
-        norm_gain.reshape(1, D),
-        nb_shard,
-        nb_row,
+        norm_gain,
+        nb_shard.T,
+        nb_row.T,
         hidden_in,
         w_self_out,
         w_cross_q,

time: 135 us -> 122 us (0.904)
  the two profiles are of different devices: /device:TPU:4 before, /device:TPU:0 now
where the time goes in v3:
time: 122 us; the launch traced here: 121 us
  Pallas kernels  119 us (98%)
  local copies, waits for them, and re-layouts  1.87 us (2%)
    pallas_call x1, Pallas kernels, per_device(): pl.pallas_call(block_kernel, out_shape=jax.ShapeDtypeStruct((SHARE, D), F...  119 us

profile of v3, /device:TPU:0, one launch (start us, length us, event | category | flops | bytes accessed | tf_op | source)
XLA Modules:
  0.0 121.2 jit_solution(11975316761595952917)
XLA Ops:
  0.0 119.3 %retro_block.1 = f32[32,4096]{1,0:T(8,128)} custom-call(bf16[256,512]{1,0:T(8,128)(2,1)} %q_ref.1, bf16[256,512]{1,0:T(8,128)(2,1)} %k_ref.1, bf16[256,512]{1,0:T(8,128)(2,1)} %v_ref.1, bf16[4096]{0:T(1024)(128)(2,1)} %gain_hbm.1, s32[2,4]{1,0:T(2,128)} %bitcast.2, s32[2,4]{1,0:T(2,128)} %bitcast.3, bf16[256,4096]{1,0:T(8,128)(2,1)} %hidden_hbm.1, ...), custom_call_target="tpu_custom_call" | custom-call | tf_op jit(solution)/shard_map/retro_block/pallas_call | solution.py:699
  119.3 1.9 %copy.15 = f32[32,4096]{1,0:T(8,128)} copy(f32[32,4096]{1,0:T(8,128)} %retro_block.1) | data formatting | bytes 1048576

commit v4 on v3

--- a/solution.py
+++ b/solution.py
@@ -257,8 +257,6 @@
 
     for k in (0, 7, 8):
         loads[k].wait()
-    for k in (1, 2, 3, 4, 5, 6, 9):
-        loads[k].start()
     first = jnp.int32(0)
     second = jnp.int32(0)
     found = jnp.int32(0)
@@ -278,7 +276,6 @@
         return arr.at[i, pl.ds((192, 192, 224)[part], (64, 32, 32)[part])]
 
     enc_sems = (es, er)
-    cross_send(enc_a, d, 12, enc_sems)
     flow_send(2, enc_b, zh, enc_sems)
     flow_send(0, enc_a, zh, enc_sems)
 
@@ -286,6 +283,7 @@
         src = at(zl, (x - dx + 4) % 4, c)
         remote(kv.at[src], kv.at[src], xs.at[dx], xr.at[dx], src, d).wait_recv()
         forward(src, dx)
+    cross_send(enc_a, d, 12, enc_sems)
     cross_send(enc_b, d, 13, enc_sems)
     for dx in (0, 1, 3, 2):
         src = at(1 - zl, (x - dx + 4) % 4, c)
@@ -297,10 +295,12 @@
             k = 4 * zz + dx
             remote(kv.at[src], kv.at[src], cs.at[k], cr.at[k], src, d).wait_recv()
 
-    gather_a_over(enc_a, enc_sems)
     gather_b_on(enc_b, enc_sems)
     flow_forward(0, enc_a, zh, enc_sems)
 
+    for k in (1, 2, 3, 4, 5, 6, 9):
+        loads[k].start()
+
     j = zl * 2 + c
 
     def block_of(i):
@@ -308,6 +308,11 @@
 
     def slot(i, carry):
         b = block_of(i)
+
+        @pl.when(i == 2)
+        def _():
+            gather_a_over(enc_a, enc_sems)
+
 
         remote(qst.at[0], qb.at[i], qs.at[0], qr.at[i], s, d).wait_recv()
         query = qb[i]
@@ -360,7 +365,6 @@
         return carry
 
     lax.fori_loop(0, 4, slot, 0)
-    gather_last_on(enc_a, enc_b, enc_sems)
     for h in range(4):
         remote(ob.at[0], ret.at[h], os_.at[0], or_.at[h], s, d).wait_recv()
         att[:, h * HD : (h + 1) * HD] = ret[h]
@@ -469,6 +473,7 @@
 
     loads[1].wait()
     scatter(att[...], wso, r1s, r1r, za1, ya1, yb1, zb1)
+    gather_last_on(enc_a, enc_b, enc_sems)
 
     loads[2].wait()
     loads[9].wait()
@@ -588,7 +593,7 @@
             cqa[rows, cols] = attend(qx[rows, cols], kx[g, :, cols], vx[g, :, cols])
         return carry
 
-    lax.fori_loop(0, 4, group, 0)
+    lax.fori_loop(0, 4, group, 0, unroll=True)
     for h in range(4):
         cols = slice(h * HD, (h + 1) * HD)
         tail = attend(qx[0:16, cols], kx[4, :, cols], vx[4, :, cols])

time: 122 us -> 117 us (0.959)
  Pallas kernels: 119 us -> 115 us
    pallas_call x1, Pallas kernels: 119 us -> 115 us  [per_device(): pl.pallas_call(block_kernel, out_shape=jax.ShapeDtypeStruct((SHARE, D), F...]
where the time goes in v4:
time: 117 us
  Pallas kernels  115 us (98%)
  local copies, waits for them, and re-layouts  1.87 us (2%)
    pallas_call x1, Pallas kernels, per_device(): pl.pallas_call(block_kernel, out_shape=jax.ShapeDtypeStruct((SHARE, D), F...  115 us

profile of v4, /device:TPU:0, one launch (start us, length us, event | category | flops | bytes accessed | tf_op | source)
XLA Modules:
  0.0 116.5 jit_solution(10339796421951527080)
XLA Ops:
  0.0 114.6 %retro_block.1 = f32[32,4096]{1,0:T(8,128)} custom-call(bf16[256,512]{1,0:T(8,128)(2,1)} %q_ref.1, bf16[256,512]{1,0:T(8,128)(2,1)} %k_ref.1, bf16[256,512]{1,0:T(8,128)(2,1)} %v_ref.1, bf16[4096]{0:T(1024)(128)(2,1)} %gain_hbm.1, s32[2,4]{1,0:T(2,128)} %bitcast.2, s32[2,4]{1,0:T(2,128)} %bitcast.3, bf16[256,4096]{1,0:T(8,128)(2,1)} %hidden_hbm.1, ...), custom_call_target="tpu_custom_call" | custom-call | tf_op jit(solution)/shard_map/retro_block/pallas_call | solution.py:704
  114.7 1.9 %copy.15 = f32[32,4096]{1,0:T(8,128)} copy(f32[32,4096]{1,0:T(8,128)} %retro_block.1) | data formatting | bytes 1048576

commit v5 on v4

--- a/solution.py
+++ b/solution.py
@@ -113,6 +113,12 @@
     r2r,
     ps,
     pr,
+    tab,
+    shard_two,
+    row_two,
+    lent,
+    ts,
+    tr,
 ):
     s = lax.axis_index("seq")
     d = lax.axis_index("db")
@@ -122,6 +128,7 @@
     y = d // 2
     zh = d % 2
     over = 2 * y + 1 - zh
+    beside = (s + 8) % 16
     far = (2, 1, 3)
 
     def at(zz, xx, cc):
@@ -154,7 +161,8 @@
         kvs[h, 0] = k_ref[:, cols]
         kvs[h, 1] = v_ref[:, cols]
         qst[h] = q_ref[:, cols]
-    pl.semaphore_wait(bar, 22)
+    pl.semaphore_signal(bar, inc=1, device_id=(beside, over), device_id_type=MESH)
+    pl.semaphore_wait(bar, 23)
 
     sends = []
 
@@ -171,6 +179,9 @@
         start(remote(kv.at[src], kv.at[src], cs.at[k], cr.at[k], at(zl, x, 1 - c), d))
 
     forward(s, 0)
+    start(remote(shard_hbm, tab.at[0], ts.at[0], tr.at[0], beside, d))
+    start(remote(row_hbm, tab.at[1], ts.at[1], tr.at[1], beside, d))
+
     low = s % 8
     high = low // 4
     j_to = (1 - high) * low + high * (7 - low)
@@ -257,15 +268,20 @@
 
     for k in (0, 7, 8):
         loads[k].wait()
-    first = jnp.int32(0)
-    second = jnp.int32(0)
-    found = jnp.int32(0)
-    for e in range(8):
-        match = shard_ref[e % 2, e // 2] == d
-        row = row_ref[e % 2, e // 2]
-        first = jnp.where(match & (found == 0), row, first)
-        second = jnp.where(match & (found == 1), row, second)
-        found = found + match.astype(jnp.int32)
+
+    def asked(shards, rows):
+        first = jnp.int32(0)
+        second = jnp.int32(0)
+        found = jnp.int32(0)
+        for e in range(8):
+            match = shards[e % 2, e // 2] == d
+            row = rows[e % 2, e // 2]
+            first = jnp.where(match & (found == 0), row, first)
+            second = jnp.where(match & (found == 1), row, second)
+            found = found + match.astype(jnp.int32)
+        return first, second
+
+    first, second = asked(shard_ref, row_ref)
     arr[d, 0:NLEN] = enc[first]
     arr[d, NLEN : 2 * NLEN] = enc[second]
 
@@ -278,12 +294,20 @@
     enc_sems = (es, er)
     flow_send(2, enc_b, zh, enc_sems)
     flow_send(0, enc_a, zh, enc_sems)
+    for k, table in ((0, shard_two), (1, row_two)):
+        remote(tab.at[k], tab.at[k], ts.at[k], tr.at[k], beside, d).wait_recv()
+        pltpu.make_async_copy(tab.at[k], table, wsem.at[10 + k]).start()
+    for k, table in ((0, shard_two), (1, row_two)):
+        pltpu.make_async_copy(tab.at[k], table, wsem.at[10 + k]).wait()
+    first, second = asked(shard_two, row_two)
+    lent[0:NLEN] = enc[first]
+    lent[NLEN:192] = enc[second, 0:64]
+    start(remote(lent, enc_a(d, 0), es.at[12], er.at[12], beside, over))
 
     for dx in (1, 3, 2):
         src = at(zl, (x - dx + 4) % 4, c)
         remote(kv.at[src], kv.at[src], xs.at[dx], xr.at[dx], src, d).wait_recv()
         forward(src, dx)
-    cross_send(enc_a, d, 12, enc_sems)
     cross_send(enc_b, d, 13, enc_sems)
     for dx in (0, 1, 3, 2):
         src = at(1 - zl, (x - dx + 4) % 4, c)
@@ -295,6 +319,7 @@
             k = 4 * zz + dx
             remote(kv.at[src], kv.at[src], cs.at[k], cr.at[k], src, d).wait_recv()
 
+    gather_a_over(enc_a, enc_sems)
     gather_b_on(enc_b, enc_sems)
     flow_forward(0, enc_a, zh, enc_sems)
 
@@ -308,10 +333,6 @@
 
     def slot(i, carry):
         b = block_of(i)
-
-        @pl.when(i == 2)
-        def _():
-            gather_a_over(enc_a, enc_sems)
 
 
         remote(qst.at[0], qb.at[i], qs.at[0], qr.at[i], s, d).wait_recv()
@@ -699,8 +720,16 @@
         pltpu.VMEM((5, 2 * NLEN, WIDTH), BF16),
         pltpu.VMEM((5, 2 * NLEN, WIDTH), BF16),
     ]
-    counts = (10, 4, 4, 4, 4, 8, 8, 4, 4, 4, 4, 17, 17, 15, 15, 17, 17, 15, 15, 2, 2)
+    counts = (12, 4, 4, 4, 4, 8, 8, 4, 4, 4, 4, 17, 17, 15, 15, 17, 17, 15, 15, 2, 2)
     scratch += [pltpu.SemaphoreType.DMA((count,)) for count in counts]
+    scratch += [
+        pltpu.VMEM((2, 2, 4), jnp.int32),
+        pltpu.SMEM((2, 4), jnp.int32),
+        pltpu.SMEM((2, 4), jnp.int32),
+        pltpu.VMEM((192, 1024), BF16),
+        pltpu.SemaphoreType.DMA((2,)),
+        pltpu.SemaphoreType.DMA((2,)),
+    ]
     return pl.pallas_call(
         block_kernel,
         out_shape=jax.ShapeDtypeStruct((SHARE, D), F32),

time: 117 us -> 111 us (0.949)
  Pallas kernels: 115 us -> 108 us
    pallas_call x1, Pallas kernels: 115 us -> 108 us  [per_device(): pl.pallas_call(block_kernel, out_shape=jax.ShapeDtypeStruct((SHARE, D), F...]
where the time goes in v5:
time: 111 us; the launch traced here: 110 us
  Pallas kernels  108 us (97%)
  local copies, waits for them, and re-layouts  1.87 us (2%)
    pallas_call x1, Pallas kernels, per_device(): pl.pallas_call(block_kernel, out_shape=jax.ShapeDtypeStruct((SHARE, D), F...  108 us

profile of v5, /device:TPU:0, one launch (start us, length us, event | category | flops | bytes accessed | tf_op | source)
XLA Modules:
  0.0 110.3 jit_solution(14149943335979708365)
XLA Ops:
  0.0 108.5 %retro_block.1 = f32[32,4096]{1,0:T(8,128)} custom-call(bf16[256,512]{1,0:T(8,128)(2,1)} %q_ref.1, bf16[256,512]{1,0:T(8,128)(2,1)} %k_ref.1, bf16[256,512]{1,0:T(8,128)(2,1)} %v_ref.1, bf16[4096]{0:T(1024)(128)(2,1)} %gain_hbm.1, s32[2,4]{1,0:T(2,128)} %bitcast.2, s32[2,4]{1,0:T(2,128)} %bitcast.3, bf16[256,4096]{1,0:T(8,128)(2,1)} %hidden_hbm.1, ...), custom_call_target="tpu_custom_call" | custom-call | tf_op jit(solution)/shard_map/retro_block/pallas_call | solution.py:733
  108.5 1.9 %copy.15 = f32[32,4096]{1,0:T(8,128)} copy(f32[32,4096]{1,0:T(8,128)} %retro_block.1) | data formatting | bytes 1048576

commit v6 on v5

--- a/solution.py
+++ b/solution.py
@@ -419,10 +419,6 @@
         spread.append(copy)
 
     def scatter(lhs, weight, send, recv, za, ya, yb, zb):
-        project_a(lhs, weight)
-        for dy in (2, 1, 3, 0):
-            yy = (y + dy) % 4
-            go(remote(part_a.at[(1 - zh) * 4 + yy], za.at[yy], send.at[dy], recv.at[dy], s, over))
         project_b(lhs, weight)
         steps = ((0, 1), (1, -1))
         for k, step in steps:
@@ -447,6 +443,10 @@
                     share_at(step, zh),
                 )
             )
+        project_a(lhs, weight)
+        for dy in (2, 1, 3, 0):
+            yy = (y + dy) % 4
+            go(remote(part_a.at[(1 - zh) * 4 + yy], za.at[yy], send.at[dy], recv.at[dy], s, over))
         for k, step in steps:
             remote(yb.at[k], yb.at[k], send.at[4 + k], recv.at[4 + k], s, d).wait_recv()
             sum_y[k] = (part_b[share_at(step, k)].astype(F32) + yb[k].astype(F32)).astype(BF16)
@@ -477,10 +477,12 @@
             + yb[5 - k, :, cols].astype(F32)
         )
 
-    def scatter_wait(send, recv, za, ya, zb):
+    def scatter_wait_a(send, recv, za, ya):
         remote(za.at[0], za.at[y], send.at[0], recv.at[0], s, over).wait_recv()
         for dy in far:
             remote(ya.at[dy], ya.at[dy], send.at[8 + dy], recv.at[8 + dy], s, d).wait_recv()
+
+    def scatter_wait_b(send, recv, zb):
         remote(zb, zb, send.at[14], recv.at[14], s, over).wait_recv()
 
     def total_of(half, cols, za, ya, yb, zb):
@@ -498,30 +500,32 @@
 
     loads[2].wait()
     loads[9].wait()
-    scatter_wait(r1s, r1r, za1, ya1, zb1)
-
-    def add_up(n, square):
-        cols = pl.ds(pl.multiple_of(n * 512, 512), 512)
-        for half in range(2):
+
+    def add_up(half):
+        def block(n, square):
+            cols = pl.ds(pl.multiple_of(n * 512, 512), 512)
             wide = pl.ds(pl.multiple_of(half * HALF + n * 512, 512), 512)
             total = total_of(half, cols, za1, ya1, yb1, zb1) + hid[:, wide].astype(F32)
             res[:, wide] = total
-            square = square + total * total
-        return square
-
-    square = lax.fori_loop(0, 4, add_up, jnp.zeros((SHARE, 512), F32))
+            return square + total * total
+
+        return block
+
+    square = jnp.zeros((SHARE, 512), F32)
+    scatter_wait_b(r1s, r1r, zb1)
+    square = lax.fori_loop(0, 4, add_up(1), square)
+    scatter_wait_a(r1s, r1r, za1, ya1)
+    square = lax.fori_loop(0, 4, add_up(0), square)
     scale = lax.rsqrt(jnp.sum(square, axis=-1, keepdims=True) / D + 1e-05)
 
-    def normalise(n, carry):
-        cols = pl.ds(pl.multiple_of(n * 512, 512), 512)
-        for half, held in enumerate((nf_a, nf_b)):
+    def normalise(half, held):
+        def block(n, carry):
+            cols = pl.ds(pl.multiple_of(n * 512, 512), 512)
             wide = pl.ds(pl.multiple_of(half * HALF + n * 512, 512), 512)
-            held[d, :, cols] = (
-                res[:, wide] * scale * gain[wide].astype(F32)
-            ).astype(BF16)
-        return carry
-
-    lax.fori_loop(0, 4, normalise, 0)
+            held[d, :, cols] = (res[:, wide] * scale * gain[wide].astype(F32)).astype(BF16)
+            return carry
+
+        lax.fori_loop(0, 4, block, 0)
 
     def share_a(i, part):
         return nf_a.at[i, pl.ds((0, 0, 16)[part], (32, 16, 16)[part])]
@@ -530,8 +534,10 @@
         return nf_b.at[i, pl.ds((0, 0, 16)[part], (32, 16, 16)[part])]
 
     ag_sems = (ags, agr)
+    normalise(1, nf_b)
+    flow_send(2, share_b, zh, ag_sems)
+    normalise(0, nf_a)
     cross_send(share_a, d, 12, ag_sems)
-    flow_send(2, share_b, zh, ag_sems)
     flow_send(0, share_a, zh, ag_sems)
     cross_send(share_b, d, 13, ag_sems)
 
@@ -595,11 +601,6 @@
     lax.fori_loop(0, 4, contract_b, 0)
     qx[...] = pltpu.roll(cqa[...].astype(BF16).astype(F32), 1, 0).astype(BF16)
 
-    @pl.when(s > 0)
-    def _():
-        remote(kx.at[4], kx.at[0], ps.at[0], pr.at[0], s, d).wait_recv()
-        remote(vx.at[4], vx.at[0], ps.at[1], pr.at[1], s, d).wait_recv()
-
     def attend(query, keys, values):
         scores = dot_nt(query, keys)
         top = jnp.max(scores, axis=-1, keepdims=True)
@@ -614,7 +615,13 @@
             cqa[rows, cols] = attend(qx[rows, cols], kx[g, :, cols], vx[g, :, cols])
         return carry
 
-    lax.fori_loop(0, 4, group, 0, unroll=True)
+    lax.fori_loop(1, 4, group, 0, unroll=True)
+    @pl.when(s > 0)
+    def _():
+        remote(kx.at[4], kx.at[0], ps.at[0], pr.at[0], s, d).wait_recv()
+        remote(vx.at[4], vx.at[0], ps.at[1], pr.at[1], s, d).wait_recv()
+
+    group(0, 0)
     for h in range(4):
         cols = slice(h * HD, (h + 1) * HD)
         tail = attend(qx[0:16, cols], kx[4, :, cols], vx[4, :, cols])
@@ -624,16 +631,20 @@
 
     loads[6].wait()
     scatter(att[...], wco, r2s, r2r, za2, ya2, yb2, zb2)
-    scatter_wait(r2s, r2r, za2, ya2, zb2)
-
-    def finish(n, carry):
-        cols = pl.ds(pl.multiple_of(n * 512, 512), 512)
-        for half in range(2):
+
+    def finish(half):
+        def block(n, carry):
+            cols = pl.ds(pl.multiple_of(n * 512, 512), 512)
             wide = pl.ds(pl.multiple_of(half * HALF + n * 512, 512), 512)
             out_ref[:, wide] = res[:, wide] + total_of(half, cols, za2, ya2, yb2, zb2)
-        return carry
-
-    lax.fori_loop(0, 4, finish, 0)
+            return carry
+
+        lax.fori_loop(0, 4, block, 0)
+
+    scatter_wait_b(r2s, r2r, zb2)
+    finish(1)
+    scatter_wait_a(r2s, r2r, za2, ya2)
+    finish(0)
 
     for copy in spread:
         copy.wait_send()

time: 111 us -> 111 us (level)
  no operation moved by 1% of the time
where the time goes in v6:
time: 111 us; the launch traced here: 110 us
  Pallas kernels  108 us (97%)
  local copies, waits for them, and re-layouts  1.87 us (2%)
    pallas_call x1, Pallas kernels, per_device(): pl.pallas_call(block_kernel, out_shape=jax.ShapeDtypeStruct((SHARE, D), F...  108 us

profile of v6, /device:TPU:0, one launch (start us, length us, event | category | flops | bytes accessed | tf_op | source)
XLA Modules:
  0.0 110.3 jit_solution(1636762902348584196)
XLA Ops:
  0.0 108.5 %retro_block.1 = f32[32,4096]{1,0:T(8,128)} custom-call(bf16[256,512]{1,0:T(8,128)(2,1)} %q_ref.1, bf16[256,512]{1,0:T(8,128)(2,1)} %k_ref.1, bf16[256,512]{1,0:T(8,128)(2,1)} %v_ref.1, bf16[4096]{0:T(1024)(128)(2,1)} %gain_hbm.1, s32[2,4]{1,0:T(2,128)} %bitcast.2, s32[2,4]{1,0:T(2,128)} %bitcast.3, bf16[256,4096]{1,0:T(8,128)(2,1)} %hidden_hbm.1, ...), custom_call_target="tpu_custom_call" | custom-call | tf_op jit(solution)/shard_map/retro_block/pallas_call | solution.py:744
  108.5 1.9 %copy.15 = f32[32,4096]{1,0:T(8,128)} copy(f32[32,4096]{1,0:T(8,128)} %retro_block.1) | data formatting | bytes 1048576

commit v7 on v6

--- a/solution.py
+++ b/solution.py
@@ -319,9 +319,9 @@
             k = 4 * zz + dx
             remote(kv.at[src], kv.at[src], cs.at[k], cr.at[k], src, d).wait_recv()
 
-    gather_a_over(enc_a, enc_sems)
     gather_b_on(enc_b, enc_sems)
     flow_forward(0, enc_a, zh, enc_sems)
+    gather_a_over(enc_a, enc_sems)
 
     for k in (1, 2, 3, 4, 5, 6, 9):
         loads[k].start()
@@ -400,7 +400,7 @@
                 ]
             return carry
 
-        lax.fori_loop(0, 4, tile, 0)
+        lax.fori_loop(0, 4, tile, 0, unroll=True)
 
     def project_b(lhs, weight):
         def tile(n, carry):
@@ -410,7 +410,7 @@
             part_b[:, :, cols] = product.reshape(8, SHARE, 512)
             return carry
 
-        lax.fori_loop(0, 4, tile, 0)
+        lax.fori_loop(0, 4, tile, 0, unroll=True)
 
     spread = []
 
@@ -513,9 +513,9 @@
 
     square = jnp.zeros((SHARE, 512), F32)
     scatter_wait_b(r1s, r1r, zb1)
-    square = lax.fori_loop(0, 4, add_up(1), square)
+    square = lax.fori_loop(0, 4, add_up(1), square, unroll=True)
     scatter_wait_a(r1s, r1r, za1, ya1)
-    square = lax.fori_loop(0, 4, add_up(0), square)
+    square = lax.fori_loop(0, 4, add_up(0), square, unroll=True)
     scale = lax.rsqrt(jnp.sum(square, axis=-1, keepdims=True) / D + 1e-05)
 
     def normalise(half, held):
@@ -525,7 +525,7 @@
             held[d, :, cols] = (res[:, wide] * scale * gain[wide].astype(F32)).astype(BF16)
             return carry
 
-        lax.fori_loop(0, 4, block, 0)
+        lax.fori_loop(0, 4, block, 0, unroll=True)
 
     def share_a(i, part):
         return nf_a.at[i, pl.ds((0, 0, 16)[part], (32, 16, 16)[part])]
@@ -596,9 +596,9 @@
         cqa[...] += dot_f32(nf_b[:, :, cols].reshape(TOK, 512), wcq[right, :])
         return carry
 
-    lax.fori_loop(0, 4, contract_a, 0)
+    lax.fori_loop(0, 4, contract_a, 0, unroll=True)
     gather_finish_b(share_b, ag_sems)
-    lax.fori_loop(0, 4, contract_b, 0)
+    lax.fori_loop(0, 4, contract_b, 0, unroll=True)
     qx[...] = pltpu.roll(cqa[...].astype(BF16).astype(F32), 1, 0).astype(BF16)
 
     def attend(query, keys, values):
@@ -639,7 +639,7 @@
             out_ref[:, wide] = res[:, wide] + total_of(half, cols, za2, ya2, yb2, zb2)
             return carry
 
-        lax.fori_loop(0, 4, block, 0)
+        lax.fori_loop(0, 4, block, 0, unroll=True)
 
     scatter_wait_b(r2s, r2r, zb2)
     finish(1)

time: 111 us -> 109 us (0.982)
    pallas_call x1, Pallas kernels: 108 us -> 107 us  [per_device(): pl.pallas_call(block_kernel, out_shape=jax.ShapeDtypeStruct((SHARE, D), F...]
where the time goes in v7:
time: 109 us; the launch traced here: 108 us
  Pallas kernels  107 us (98%)
  local copies, waits for them, and re-layouts  1.87 us (2%)
    pallas_call x1, Pallas kernels, per_device(): pl.pallas_call(block_kernel, out_shape=jax.ShapeDtypeStruct((SHARE, D), F...  107 us

profile of v7, /device:TPU:0, one launch (start us, length us, event | category | flops | bytes accessed | tf_op | source)
XLA Modules:
  0.0 108.4 jit_solution(2178499322767731161)
XLA Ops:
  0.0 106.6 %retro_block.1 = f32[32,4096]{1,0:T(8,128)} custom-call(bf16[256,512]{1,0:T(8,128)(2,1)} %q_ref.1, bf16[256,512]{1,0:T(8,128)(2,1)} %k_ref.1, bf16[256,512]{1,0:T(8,128)(2,1)} %v_ref.1, bf16[4096]{0:T(1024)(128)(2,1)} %gain_hbm.1, s32[2,4]{1,0:T(2,128)} %bitcast.2, s32[2,4]{1,0:T(2,128)} %bitcast.3, bf16[256,4096]{1,0:T(8,128)(2,1)} %hidden_hbm.1, ...), custom_call_target="tpu_custom_call" | custom-call | tf_op jit(solution)/shard_map/retro_block/pallas_call | solution.py:744
  106.6 1.9 %copy.15 = f32[32,4096]{1,0:T(8,128)} copy(f32[32,4096]{1,0:T(8,128)} %retro_block.1) | data formatting | bytes 1048576

commit v8 on v7

--- a/solution.py
+++ b/solution.py
@@ -546,18 +546,19 @@
     loads[3].wait()
     loads[4].wait()
 
-    def cross_pair(e):
+    def entry_of(e):
         shard = shard_ref[e % 2, e // 2]
         rank = jnp.int32(0)
         for earlier in range(e):
             rank = rank + (shard_ref[earlier % 2, earlier // 2] == shard).astype(jnp.int32)
-        entry = arr.reshape(16, NLEN, 1024)[shard * 2 + jnp.minimum(rank, 1)]
-        rows = slice((e % 2) * NLEN, (e % 2 + 1) * NLEN)
-        kx[e // 2 + 1, rows, :] = dot_f32(entry, wck[...]).astype(BF16)
-        vx[e // 2 + 1, rows, :] = dot_f32(entry, wcv[...]).astype(BF16)
-
-    cross_pair(6)
-    cross_pair(7)
+        return arr.reshape(16, NLEN, 1024)[shard * 2 + jnp.minimum(rank, 1)]
+
+    def cross_span(u):
+        entries = jnp.concatenate((entry_of(2 * u), entry_of(2 * u + 1)))
+        kx[u + 1] = dot_f32(entries, wck[...]).astype(BF16)
+        vx[u + 1] = dot_f32(entries, wcv[...]).astype(BF16)
+
+    cross_span(3)
 
     @pl.when(s < 15)
     def _():
@@ -572,11 +573,10 @@
     gather_a_over(share_a, ag_sems)
     gather_b_on(share_b, ag_sems)
     flow_forward(0, share_a, zh, ag_sems)
-    for e in range(4):
-        cross_pair(e)
+    cross_span(0)
+    cross_span(1)
     gather_last_on(share_a, share_b, ag_sems)
-    for e in range(4, 6):
-        cross_pair(e)
+    cross_span(2)
     for copy in spread:
         copy.wait_send()
     spread.clear()

time: 109 us -> 109 us (level)
  no operation moved by 1% of the time
where the time goes in v8:
time: 109 us; the launch traced here: 108 us
  Pallas kernels  107 us (98%)
  local copies, waits for them, and re-layouts  1.87 us (2%)
    pallas_call x1, Pallas kernels, per_device(): pl.pallas_call(block_kernel, out_shape=jax.ShapeDtypeStruct((SHARE, D), F...  107 us

profile of v8, /device:TPU:0, one launch (start us, length us, event | category | flops | bytes accessed | tf_op | source)
XLA Modules:
  0.0 108.4 jit_solution(61151067164693539)
XLA Ops:
  0.0 106.6 %retro_block.1 = f32[32,4096]{1,0:T(8,128)} custom-call(bf16[256,512]{1,0:T(8,128)(2,1)} %q_ref.1, bf16[256,512]{1,0:T(8,128)(2,1)} %k_ref.1, bf16[256,512]{1,0:T(8,128)(2,1)} %v_ref.1, bf16[4096]{0:T(1024)(128)(2,1)} %gain_hbm.1, s32[2,4]{1,0:T(2,128)} %bitcast.2, s32[2,4]{1,0:T(2,128)} %bitcast.3, bf16[256,4096]{1,0:T(8,128)(2,1)} %hidden_hbm.1, ...), custom_call_target="tpu_custom_call" | custom-call | tf_op jit(solution)/shard_map/retro_block/pallas_call | solution.py:744
  106.6 1.9 %copy.15 = f32[32,4096]{1,0:T(8,128)} copy(f32[32,4096]{1,0:T(8,128)} %retro_block.1) | data formatting | bytes 1048576
